TPU v7x, 512 devices: a whole 4x4x16 slice. The times are simulated.
512 devices in a mesh: head: 16 (over z), ctx: 32 (over x, y, core).
Axes of the slice: x: 4, y: 4, z: 16, core: 2. Of those that a mesh axis runs over, the one named last changes fastest.
Arguments:
- head_inputs: bfloat16 [32768, 8192], P('ctx', 'head'), may hold values from -6 to 6
- gate_z: bfloat16 [32768, 8192], P('ctx', 'head'), may hold values from -6 to 6
- input_b: bfloat16 [32768, 1024], P('ctx'), may hold values from -0.039794922 to 0.039794922
- output_c: bfloat16 [32768, 1024], P('ctx'), may hold values from -6 to 6
- log_decay: float32 [32768, 128], P('ctx', 'head'), may hold values from -1 to 0
- lengths: int32 [16], replicated, may hold values from 1 to 8192, 32768 in all
- skip_coef: float32 [128], P('head'), may hold values from 0.5 to 1.5
- norm_gain: float32 [8192], P('head'), may hold values from 0.5 to 1.5
Outputs:
- normed: bfloat16 [32768, 8192], P('ctx', 'head')
Inputs may be any that keep to these rules, and one draw needn't show every extreme that they name: `lengths`: requests lie end to end from token 0 and fill all 32768 tokens; the longest has exactly 8192 tokens.
All inputs are finite; a program needn't handle non-finite values.
Results may differ from a plain program's by a relative error of at most 0.0085.
Values sent between devices are 32-bit elements; how exact they have to be, the bound alone decides.
A program may use at most 64 MiB of HBM per device.

v0:
```python
import jax
import jax.numpy as jnp
from jax import lax
from jax.sharding import PartitionSpec as P

HEAD_COUNT = 128
G = 8
BLOCK = 512


def from_behind(block, axis, distance):
    devices = range(lax.axis_size(axis))
    route = [(i - distance, i) for i in devices if i - distance in devices]
    return lax.ppermute(block, axis, route)


def segments_of(starts, positions):
    return jnp.sum((starts[None, :] <= positions[:, None]).astype(jnp.int32), axis=1) - 1


def on_device(head_inputs, gate_z, input_b, output_c, log_decay, lengths, skip_coef, norm_gain):
    tok_local = head_inputs.shape[0]
    heads_local = skip_coef.shape[0]
    width = head_inputs.shape[1] // heads_local
    state_size = input_b.shape[1] // G
    per_group = HEAD_COUNT // G
    head_pos = lax.axis_index("head")
    ctx_pos = lax.axis_index("ctx")
    groups_local = 1
    first_group = head_pos * heads_local // per_group
    heads_per = heads_local // groups_local
    bmaps_local = lax.dynamic_slice_in_dim(
        input_b, first_group * state_size, groups_local * state_size, 1
    )
    cmaps_local = lax.dynamic_slice_in_dim(
        output_c, first_group * state_size, groups_local * state_size, 1
    )
    bmaps_local = bmaps_local.reshape(tok_local, groups_local, state_size)
    cmaps_local = cmaps_local.reshape(tok_local, groups_local, state_size)
    starts = jnp.cumsum(lengths) - lengths
    positions = ctx_pos * tok_local + jnp.arange(tok_local, dtype=jnp.int32)
    request_of = segments_of(starts, positions)
    before_request = segments_of(starts, (ctx_pos * tok_local - 1).reshape(1))
    blocks = tok_local // BLOCK
    request_blocks = request_of.reshape(blocks, BLOCK)
    prior_requests = jnp.concatenate([before_request, request_blocks[:-1, -1]])
    inputs_blocks = head_inputs.reshape(blocks, BLOCK, heads_local, width)
    bmaps_blocks = bmaps_local.reshape(blocks, BLOCK, groups_local, state_size)
    cmaps_blocks = cmaps_local.reshape(blocks, BLOCK, groups_local, state_size)
    decay_blocks = log_decay.reshape(blocks, BLOCK, heads_local)
    lower_mask = jnp.arange(BLOCK)[:, None] >= jnp.arange(BLOCK)[None, :]

    def block_terms(element):
        inputs_block, bmaps_block, cmaps_block, decay_block, request_block, prior_request = element
        cum_decay = jnp.cumsum(decay_block, axis=0).T
        visible = (request_block[:, None] == request_block[None, :]) & lower_mask
        gaps = cum_decay[:, :, None] - cum_decay[:, None, :]
        decay_matrix = jnp.exp(jnp.where(visible[None], gaps, -jnp.inf))
        scores = jnp.einsum(
            "tgn,sgn->gts", cmaps_block, bmaps_block, preferred_element_type=jnp.float32
        )
        weights = decay_matrix.reshape(groups_local, heads_per, BLOCK, BLOCK) * scores[:, None]
        weights = weights.reshape(heads_local, BLOCK, BLOCK).astype(jnp.bfloat16)
        inner_part = jnp.einsum(
            "hts,shp->thp", weights, inputs_block, preferred_element_type=jnp.float32
        )
        live_end = request_block == request_block[-1]
        end_weight = jnp.where(live_end[None, :], jnp.exp(cum_decay[:, -1:] - cum_decay), 0.0)
        wide_bmaps = jnp.broadcast_to(
            bmaps_block[:, :, None, :], (BLOCK, groups_local, heads_per, state_size)
        )
        wide_bmaps = wide_bmaps.reshape(BLOCK, heads_local, state_size)
        scaled = (end_weight.T[:, :, None] * wide_bmaps).astype(jnp.bfloat16)
        block_state = jnp.einsum(
            "shn,shp->hpn", scaled, inputs_block, preferred_element_type=jnp.float32
        )
        block_decay = jnp.where(request_block[-1] == prior_request, jnp.exp(cum_decay[:, -1]), 0.0)
        carry_coef = jnp.where((request_block == prior_request)[:, None], jnp.exp(cum_decay.T), 0.0)
        return (inner_part, block_state, block_decay, carry_coef)

    inner_part, block_states, block_decays, carry_coefs = lax.map(
        block_terms,
        (inputs_blocks, bmaps_blocks, cmaps_blocks, decay_blocks, request_blocks, prior_requests),
    )

    def local_prefix(running, element):
        run_decay, run_state = running
        block_decay, block_state = element
        advanced = (run_decay * block_decay, block_decay[:, None, None] * run_state + block_state)
        return (advanced, running)

    start_carry = (
        jnp.ones((heads_local,), jnp.float32),
        jnp.zeros((heads_local, width, state_size), jnp.float32),
    )
    (device_decay, device_state), (before_decay, before_state) = lax.scan(
        local_prefix, start_carry, (block_decays, block_states)
    )

    def apply_cmaps(cmaps, states):
        grouped = states.reshape(groups_local, heads_per, width, state_size)
        applied = jnp.einsum(
            "qgn,gkpn->qgkp", cmaps.astype(jnp.float32), grouped, precision=lax.Precision.HIGHEST
        )
        return applied.reshape(cmaps.shape[0], heads_local, width)

    def advance(counter, carried_pair):
        received, sending = carried_pair
        arrived = from_behind(sending, "ctx", 1)
        return (arrived, device_decay[:, None, None] * arrived + device_state)

    zero_state = jnp.zeros((heads_local, width, state_size), jnp.float32)
    incoming, leftover = lax.fori_loop(
        0, lax.axis_size("ctx") - 1, advance, (zero_state, device_state)
    )
    entering = before_decay[:, :, None, None] * incoming[None] + before_state
    carried = lax.map(lambda element: apply_cmaps(element[0], element[1]), (cmaps_blocks, entering))
    carried = carry_coefs[:, :, :, None] * carried
    ssd_output = (
        inner_part + skip_coef[None, None, :, None] * inputs_blocks.astype(jnp.float32) + carried
    )
    ssd_output = ssd_output.reshape(tok_local, heads_local * width).astype(jnp.bfloat16)
    gated_output = ssd_output.astype(jnp.float32) * jax.nn.silu(gate_z.astype(jnp.float32))
    partial_squares = jnp.sum(gated_output * gated_output, axis=1)
    total_squares = lax.psum(partial_squares, "head")
    mean_square = total_squares / (HEAD_COUNT * width)
    normed = gated_output * lax.rsqrt(mean_square + 1e-05)[:, None]
    normed = normed * norm_gain[None, :]
    return normed.astype(jnp.bfloat16)


def solution(mesh):
    return jax.shard_map(
        on_device,
        mesh=mesh,
        in_specs=(
            P("ctx", "head"),
            P("ctx", "head"),
            P("ctx", None),
            P("ctx", None),
            P("ctx", "head"),
            P(),
            P("head"),
            P("head"),
        ),
        out_specs=P("ctx", "head"),
        check_vma=False,
    )
```

profile of v0, /device:TPU:6, one launch (start us, length us, event | category | flops | bytes accessed | tf_op | source)
XLA Modules:
  0.0 415.8 jit_solution(664432653916026506)
XLA Ops:
  5.5 2.8 reshape.197
  8.2 2.2 copy.48
  11.2 23.2 %while.58 = (s32[]{:T(128)}, f32[2,512,8,64]{1,3,2,0:T(8,128)S(1)}, f32[2,8,64,128]{3,2,1,0:T(8,128)S(1)}, f32[2,8]{1,0:T(2,128)S(1)}, f32[2,512,8]{1,2,0:T(8,12...) while((s32[]{:T(128)}, f32[2,512,8,64]{1,3,2,0:T(8,128)S(1)}, ...), condition=%wide.region_6.7_spmd.clone, body=%wide.region_3.6_spmd.clone.sunk | while | flops 413480064 | bytes 6111423 | solution.py:81
  15.7 3.6 fusion.60
  27.3 3.6 fusion.60
  37.1 325.3 %while.56 = (s32[]{:T(128)}, f32[8,64,128]{2,1,0:T(8,128)}, f32[8,64,128]{2,1,0:T(8,128)S(1)}, f32[8]{0:T(128)S(1)}, f32[8,64,128]{2,1,0:T(8,128)S(1)}, /*index=5*/s32[]{:T(128)}) while((s32[]{:T(128)}, f32[8,64,128]{2,1,0:T(8,128)}, f32[8,64,128]{2,1,0:T(8,128)S(1)}, f32[8]{0:T(128)S(1)}, f32[8,64,128]{2,1,0:T(8,128)S(1)}, ...), condition=%wide.region_10.11_spmd, body=%wide.region_9.10_spmd.sunk | while | flops 131074 | bytes 2883753 | solution.py:113
  37.1 1.9 collective-permute-start
  39.0 7.9 %collective-permute-done = f32[8,64,128]{2,1,0:T(8,128)S(1)} collective-permute-done((f32[8,64,128]{2,1,0:T(8,128)S(1)}, f32[8,64,128]{2,1,0:T(8,128)S(1)}, u32[]{:S(2)}, u32[]{:S(2)}) %collective-permute-start) | collective-permute-done | bytes 262176 | tf_op jit(solution)/shard_map/while/body/eval_jaxpr/ppermute | solution.py:14
  47.6 1.9 collective-permute-start
  49.5 7.9 %collective-permute-done = f32[8,64,128]{2,1,0:T(8,128)S(1)} collective-permute-done((f32[8,64,128]{2,1,0:T(8,128)S(1)}, f32[8,64,128]{2,1,0:T(8,128)S(1)}, u32[]{:S(2)}, u32[]{:S(2)}) %collective-permute-start) | collective-permute-done | bytes 262176 | tf_op jit(solution)/shard_map/while/body/eval_jaxpr/ppermute | solution.py:14
  58.1 1.9 collective-permute-start
  60.0 7.9 %collective-permute-done = f32[8,64,128]{2,1,0:T(8,128)S(1)} collective-permute-done((f32[8,64,128]{2,1,0:T(8,128)S(1)}, f32[8,64,128]{2,1,0:T(8,128)S(1)}, u32[]{:S(2)}, u32[]{:S(2)}) %collective-permute-start) | collective-permute-done | bytes 262176 | tf_op jit(solution)/shard_map/while/body/eval_jaxpr/ppermute | solution.py:14
  68.6 1.9 collective-permute-start
  70.5 7.9 %collective-permute-done = f32[8,64,128]{2,1,0:T(8,128)S(1)} collective-permute-done((f32[8,64,128]{2,1,0:T(8,128)S(1)}, f32[8,64,128]{2,1,0:T(8,128)S(1)}, u32[]{:S(2)}, u32[]{:S(2)}) %collective-permute-start) | collective-permute-done | bytes 262176 | tf_op jit(solution)/shard_map/while/body/eval_jaxpr/ppermute | solution.py:14
  79.1 1.9 collective-permute-start
  81.0 7.9 %collective-permute-done = f32[8,64,128]{2,1,0:T(8,128)S(1)} collective-permute-done((f32[8,64,128]{2,1,0:T(8,128)S(1)}, f32[8,64,128]{2,1,0:T(8,128)S(1)}, u32[]{:S(2)}, u32[]{:S(2)}) %collective-permute-start) | collective-permute-done | bytes 262176 | tf_op jit(solution)/shard_map/while/body/eval_jaxpr/ppermute | solution.py:14
  89.6 1.9 collective-permute-start
  91.5 7.9 %collective-permute-done = f32[8,64,128]{2,1,0:T(8,128)S(1)} collective-permute-done((f32[8,64,128]{2,1,0:T(8,128)S(1)}, f32[8,64,128]{2,1,0:T(8,128)S(1)}, u32[]{:S(2)}, u32[]{:S(2)}) %collective-permute-start) | collective-permute-done | bytes 262176 | tf_op jit(solution)/shard_map/while/body/eval_jaxpr/ppermute | solution.py:14
  102.0 7.9 %collective-permute-done = f32[8,64,128]{2,1,0:T(8,128)S(1)} collective-permute-done((f32[8,64,128]{2,1,0:T(8,128)S(1)}, f32[8,64,128]{2,1,0:T(8,128)S(1)}, u32[]{:S(2)}, u32[]{:S(2)}) %collective-permute-start) | collective-permute-done | bytes 262176 | tf_op jit(solution)/shard_map/while/body/eval_jaxpr/ppermute | solution.py:14
  112.5 7.9 %collective-permute-done = f32[8,64,128]{2,1,0:T(8,128)S(1)} collective-permute-done((f32[8,64,128]{2,1,0:T(8,128)S(1)}, f32[8,64,128]{2,1,0:T(8,128)S(1)}, u32[]{:S(2)}, u32[]{:S(2)}) %collective-permute-start) | collective-permute-done | bytes 262176 | tf_op jit(solution)/shard_map/while/body/eval_jaxpr/ppermute | solution.py:14
  123.0 7.9 %collective-permute-done = f32[8,64,128]{2,1,0:T(8,128)S(1)} collective-permute-done((f32[8,64,128]{2,1,0:T(8,128)S(1)}, f32[8,64,128]{2,1,0:T(8,128)S(1)}, u32[]{:S(2)}, u32[]{:S(2)}) %collective-permute-start) | collective-permute-done | bytes 262176 | tf_op jit(solution)/shard_map/while/body/eval_jaxpr/ppermute | solution.py:14
  133.4 7.9 %collective-permute-done = f32[8,64,128]{2,1,0:T(8,128)S(1)} collective-permute-done((f32[8,64,128]{2,1,0:T(8,128)S(1)}, f32[8,64,128]{2,1,0:T(8,128)S(1)}, u32[]{:S(2)}, u32[]{:S(2)}) %collective-permute-start) | collective-permute-done | bytes 262176 | tf_op jit(solution)/shard_map/while/body/eval_jaxpr/ppermute | solution.py:14
  143.9 7.9 %collective-permute-done = f32[8,64,128]{2,1,0:T(8,128)S(1)} collective-permute-done((f32[8,64,128]{2,1,0:T(8,128)S(1)}, f32[8,64,128]{2,1,0:T(8,128)S(1)}, u32[]{:S(2)}, u32[]{:S(2)}) %collective-permute-start) | collective-permute-done | bytes 262176 | tf_op jit(solution)/shard_map/while/body/eval_jaxpr/ppermute | solution.py:14
  154.4 7.9 %collective-permute-done = f32[8,64,128]{2,1,0:T(8,128)S(1)} collective-permute-done((f32[8,64,128]{2,1,0:T(8,128)S(1)}, f32[8,64,128]{2,1,0:T(8,128)S(1)}, u32[]{:S(2)}, u32[]{:S(2)}) %collective-permute-start) | collective-permute-done | bytes 262176 | tf_op jit(solution)/shard_map/while/body/eval_jaxpr/ppermute | solution.py:14
  164.9 7.9 %collective-permute-done = f32[8,64,128]{2,1,0:T(8,128)S(1)} collective-permute-done((f32[8,64,128]{2,1,0:T(8,128)S(1)}, f32[8,64,128]{2,1,0:T(8,128)S(1)}, u32[]{:S(2)}, u32[]{:S(2)}) %collective-permute-start) | collective-permute-done | bytes 262176 | tf_op jit(solution)/shard_map/while/body/eval_jaxpr/ppermute | solution.py:14
  175.4 7.9 %collective-permute-done = f32[8,64,128]{2,1,0:T(8,128)S(1)} collective-permute-done((f32[8,64,128]{2,1,0:T(8,128)S(1)}, f32[8,64,128]{2,1,0:T(8,128)S(1)}, u32[]{:S(2)}, u32[]{:S(2)}) %collective-permute-start) | collective-permute-done | bytes 262176 | tf_op jit(solution)/shard_map/while/body/eval_jaxpr/ppermute | solution.py:14
  185.9 7.9 %collective-permute-done = f32[8,64,128]{2,1,0:T(8,128)S(1)} collective-permute-done((f32[8,64,128]{2,1,0:T(8,128)S(1)}, f32[8,64,128]{2,1,0:T(8,128)S(1)}, u32[]{:S(2)}, u32[]{:S(2)}) %collective-permute-start) | collective-permute-done | bytes 262176 | tf_op jit(solution)/shard_map/while/body/eval_jaxpr/ppermute | solution.py:14
  196.4 7.9 %collective-permute-done = f32[8,64,128]{2,1,0:T(8,128)S(1)} collective-permute-done((f32[8,64,128]{2,1,0:T(8,128)S(1)}, f32[8,64,128]{2,1,0:T(8,128)S(1)}, u32[]{:S(2)}, u32[]{:S(2)}) %collective-permute-start) | collective-permute-done | bytes 262176 | tf_op jit(solution)/shard_map/while/body/eval_jaxpr/ppermute | solution.py:14
  205.0 1.9 collective-permute-start
  206.9 7.9 %collective-permute-done = f32[8,64,128]{2,1,0:T(8,128)S(1)} collective-permute-done((f32[8,64,128]{2,1,0:T(8,128)S(1)}, f32[8,64,128]{2,1,0:T(8,128)S(1)}, u32[]{:S(2)}, u32[]{:S(2)}) %collective-permute-start) | collective-permute-done | bytes 262176 | tf_op jit(solution)/shard_map/while/body/eval_jaxpr/ppermute | solution.py:14
  217.4 7.9 %collective-permute-done = f32[8,64,128]{2,1,0:T(8,128)S(1)} collective-permute-done((f32[8,64,128]{2,1,0:T(8,128)S(1)}, f32[8,64,128]{2,1,0:T(8,128)S(1)}, u32[]{:S(2)}, u32[]{:S(2)}) %collective-permute-start) | collective-permute-done | bytes 262176 | tf_op jit(solution)/shard_map/while/body/eval_jaxpr/ppermute | solution.py:14
  227.9 7.9 %collective-permute-done = f32[8,64,128]{2,1,0:T(8,128)S(1)} collective-permute-done((f32[8,64,128]{2,1,0:T(8,128)S(1)}, f32[8,64,128]{2,1,0:T(8,128)S(1)}, u32[]{:S(2)}, u32[]{:S(2)}) %collective-permute-start) | collective-permute-done | bytes 262176 | tf_op jit(solution)/shard_map/while/body/eval_jaxpr/ppermute | solution.py:14
  238.4 7.9 %collective-permute-done = f32[8,64,128]{2,1,0:T(8,128)S(1)} collective-permute-done((f32[8,64,128]{2,1,0:T(8,128)S(1)}, f32[8,64,128]{2,1,0:T(8,128)S(1)}, u32[]{:S(2)}, u32[]{:S(2)}) %collective-permute-start) | collective-permute-done | bytes 262176 | tf_op jit(solution)/shard_map/while/body/eval_jaxpr/ppermute | solution.py:14
  248.8 7.9 %collective-permute-done = f32[8,64,128]{2,1,0:T(8,128)S(1)} collective-permute-done((f32[8,64,128]{2,1,0:T(8,128)S(1)}, f32[8,64,128]{2,1,0:T(8,128)S(1)}, u32[]{:S(2)}, u32[]{:S(2)}) %collective-permute-start) | collective-permute-done | bytes 262176 | tf_op jit(solution)/shard_map/while/body/eval_jaxpr/ppermute | solution.py:14
  259.3 7.9 %collective-permute-done = f32[8,64,128]{2,1,0:T(8,128)S(1)} collective-permute-done((f32[8,64,128]{2,1,0:T(8,128)S(1)}, f32[8,64,128]{2,1,0:T(8,128)S(1)}, u32[]{:S(2)}, u32[]{:S(2)}) %collective-permute-start) | collective-permute-done | bytes 262176 | tf_op jit(solution)/shard_map/while/body/eval_jaxpr/ppermute | solution.py:14
  269.8 7.9 %collective-permute-done = f32[8,64,128]{2,1,0:T(8,128)S(1)} collective-permute-done((f32[8,64,128]{2,1,0:T(8,128)S(1)}, f32[8,64,128]{2,1,0:T(8,128)S(1)}, u32[]{:S(2)}, u32[]{:S(2)}) %collective-permute-start) | collective-permute-done | bytes 262176 | tf_op jit(solution)/shard_map/while/body/eval_jaxpr/ppermute | solution.py:14
  280.3 7.9 %collective-permute-done = f32[8,64,128]{2,1,0:T(8,128)S(1)} collective-permute-done((f32[8,64,128]{2,1,0:T(8,128)S(1)}, f32[8,64,128]{2,1,0:T(8,128)S(1)}, u32[]{:S(2)}, u32[]{:S(2)}) %collective-permute-start) | collective-permute-done | bytes 262176 | tf_op jit(solution)/shard_map/while/body/eval_jaxpr/ppermute | solution.py:14
  290.8 7.9 %collective-permute-done = f32[8,64,128]{2,1,0:T(8,128)S(1)} collective-permute-done((f32[8,64,128]{2,1,0:T(8,128)S(1)}, f32[8,64,128]{2,1,0:T(8,128)S(1)}, u32[]{:S(2)}, u32[]{:S(2)}) %collective-permute-start) | collective-permute-done | bytes 262176 | tf_op jit(solution)/shard_map/while/body/eval_jaxpr/ppermute | solution.py:14
  301.3 7.9 %collective-permute-done = f32[8,64,128]{2,1,0:T(8,128)S(1)} collective-permute-done((f32[8,64,128]{2,1,0:T(8,128)S(1)}, f32[8,64,128]{2,1,0:T(8,128)S(1)}, u32[]{:S(2)}, u32[]{:S(2)}) %collective-permute-start) | collective-permute-done | bytes 262176 | tf_op jit(solution)/shard_map/while/body/eval_jaxpr/ppermute | solution.py:14
  311.8 7.9 %collective-permute-done = f32[8,64,128]{2,1,0:T(8,128)S(1)} collective-permute-done((f32[8,64,128]{2,1,0:T(8,128)S(1)}, f32[8,64,128]{2,1,0:T(8,128)S(1)}, u32[]{:S(2)}, u32[]{:S(2)}) %collective-permute-start) | collective-permute-done | bytes 262176 | tf_op jit(solution)/shard_map/while/body/eval_jaxpr/ppermute | solution.py:14
  322.3 7.9 %collective-permute-done = f32[8,64,128]{2,1,0:T(8,128)S(1)} collective-permute-done((f32[8,64,128]{2,1,0:T(8,128)S(1)}, f32[8,64,128]{2,1,0:T(8,128)S(1)}, u32[]{:S(2)}, u32[]{:S(2)}) %collective-permute-start) | collective-permute-done | bytes 262176 | tf_op jit(solution)/shard_map/while/body/eval_jaxpr/ppermute | solution.py:14
  332.8 7.9 %collective-permute-done = f32[8,64,128]{2,1,0:T(8,128)S(1)} collective-permute-done((f32[8,64,128]{2,1,0:T(8,128)S(1)}, f32[8,64,128]{2,1,0:T(8,128)S(1)}, u32[]{:S(2)}, u32[]{:S(2)}) %collective-permute-start) | collective-permute-done | bytes 262176 | tf_op jit(solution)/shard_map/while/body/eval_jaxpr/ppermute | solution.py:14
  343.3 7.9 %collective-permute-done = f32[8,64,128]{2,1,0:T(8,128)S(1)} collective-permute-done((f32[8,64,128]{2,1,0:T(8,128)S(1)}, f32[8,64,128]{2,1,0:T(8,128)S(1)}, u32[]{:S(2)}, u32[]{:S(2)}) %collective-permute-start) | collective-permute-done | bytes 262176 | tf_op jit(solution)/shard_map/while/body/eval_jaxpr/ppermute | solution.py:14
  353.8 7.9 %collective-permute-done = f32[8,64,128]{2,1,0:T(8,128)S(1)} collective-permute-done((f32[8,64,128]{2,1,0:T(8,128)S(1)}, f32[8,64,128]{2,1,0:T(8,128)S(1)}, u32[]{:S(2)}, u32[]{:S(2)}) %collective-permute-start) | collective-permute-done | bytes 262176 | tf_op jit(solution)/shard_map/while/body/eval_jaxpr/ppermute | solution.py:14
  365.2 3.2 while.57
  368.4 2.5 fusion.36
  375.3 36.5 %psum.7 = f32[1024]{0:T(1024)S(1)} all-reduce(f32[1024]{0:T(1024)S(1)} %multiply_reduce_fusion), channel_id=1, replica_groups=mesh['head'=16,'ctx'=32] {'head'}, use_global_device_ids=true, to_apply=%region_14.15 | all-reduce | flops 1024 | bytes 8192 | tf_op jit(solution)/shard_map/psum | solution.py:125
  413.5 2.3 copy.54
  (197 shorter events, 102.7 us)
Async XLA Ops:
  10.5 0.8 copy-start.1
  37.1 9.8 %collective-permute-start = (f32[8,64,128]{2,1,0:T(8,128)S(1)}, f32[8,64,128]{2,1,0:T(8,128)S(1)}, u32[]{:S(2)}, u32[]{:S(2)}) collective-permute-start(f32[8,64,128]{2,1,0:T(8,128)S(1)} %get-tuple-element.609), channel_id=1, source_target_pairs={{0,1},{1,2},{2,3},{3,4},{4,5},{5,6},{6,7},{7,8},{8,9},{9,10},{10,1... | collective-permute-start | bytes 786440 | tf_op jit(solution)/shard_map/while/body/eval_jaxpr/ppermute | solution.py:14
  46.9 0.7 copy-start
  47.6 9.8 %collective-permute-start = (f32[8,64,128]{2,1,0:T(8,128)S(1)}, f32[8,64,128]{2,1,0:T(8,128)S(1)}, u32[]{:S(2)}, u32[]{:S(2)}) collective-permute-start(f32[8,64,128]{2,1,0:T(8,128)S(1)} %get-tuple-element.609), channel_id=1, source_target_pairs={{0,1},{1,2},{2,3},{3,4},{4,5},{5,6},{6,7},{7,8},{8,9},{9,10},{10,1... | collective-permute-start | bytes 786440 | tf_op jit(solution)/shard_map/while/body/eval_jaxpr/ppermute | solution.py:14
  57.4 0.7 copy-start
  58.1 9.8 %collective-permute-start = (f32[8,64,128]{2,1,0:T(8,128)S(1)}, f32[8,64,128]{2,1,0:T(8,128)S(1)}, u32[]{:S(2)}, u32[]{:S(2)}) collective-permute-start(f32[8,64,128]{2,1,0:T(8,128)S(1)} %get-tuple-element.609), channel_id=1, source_target_pairs={{0,1},{1,2},{2,3},{3,4},{4,5},{5,6},{6,7},{7,8},{8,9},{9,10},{10,1... | collective-permute-start | bytes 786440 | tf_op jit(solution)/shard_map/while/body/eval_jaxpr/ppermute | solution.py:14
  67.9 0.7 copy-start
  68.6 9.8 %collective-permute-start = (f32[8,64,128]{2,1,0:T(8,128)S(1)}, f32[8,64,128]{2,1,0:T(8,128)S(1)}, u32[]{:S(2)}, u32[]{:S(2)}) collective-permute-start(f32[8,64,128]{2,1,0:T(8,128)S(1)} %get-tuple-element.609), channel_id=1, source_target_pairs={{0,1},{1,2},{2,3},{3,4},{4,5},{5,6},{6,7},{7,8},{8,9},{9,10},{10,1... | collective-permute-start | bytes 786440 | tf_op jit(solution)/shard_map/while/body/eval_jaxpr/ppermute | solution.py:14
  78.4 0.7 copy-start
  79.1 9.8 %collective-permute-start = (f32[8,64,128]{2,1,0:T(8,128)S(1)}, f32[8,64,128]{2,1,0:T(8,128)S(1)}, u32[]{:S(2)}, u32[]{:S(2)}) collective-permute-start(f32[8,64,128]{2,1,0:T(8,128)S(1)} %get-tuple-element.609), channel_id=1, source_target_pairs={{0,1},{1,2},{2,3},{3,4},{4,5},{5,6},{6,7},{7,8},{8,9},{9,10},{10,1... | collective-permute-start | bytes 786440 | tf_op jit(solution)/shard_map/while/body/eval_jaxpr/ppermute | solution.py:14
  88.9 0.7 copy-start
  89.6 9.8 %collective-permute-start = (f32[8,64,128]{2,1,0:T(8,128)S(1)}, f32[8,64,128]{2,1,0:T(8,128)S(1)}, u32[]{:S(2)}, u32[]{:S(2)}) collective-permute-start(f32[8,64,128]{2,1,0:T(8,128)S(1)} %get-tuple-element.609), channel_id=1, source_target_pairs={{0,1},{1,2},{2,3},{3,4},{4,5},{5,6},{6,7},{7,8},{8,9},{9,10},{10,1... | collective-permute-start | bytes 786440 | tf_op jit(solution)/shard_map/while/body/eval_jaxpr/ppermute | solution.py:14
  99.3 0.7 copy-start
  100.1 9.8 %collective-permute-start = (f32[8,64,128]{2,1,0:T(8,128)S(1)}, f32[8,64,128]{2,1,0:T(8,128)S(1)}, u32[]{:S(2)}, u32[]{:S(2)}) collective-permute-start(f32[8,64,128]{2,1,0:T(8,128)S(1)} %get-tuple-element.609), channel_id=1, source_target_pairs={{0,1},{1,2},{2,3},{3,4},{4,5},{5,6},{6,7},{7,8},{8,9},{9,10},{10,1... | collective-permute-start | bytes 786440 | tf_op jit(solution)/shard_map/while/body/eval_jaxpr/ppermute | solution.py:14
  109.8 0.7 copy-start
  110.5 9.8 %collective-permute-start = (f32[8,64,128]{2,1,0:T(8,128)S(1)}, f32[8,64,128]{2,1,0:T(8,128)S(1)}, u32[]{:S(2)}, u32[]{:S(2)}) collective-permute-start(f32[8,64,128]{2,1,0:T(8,128)S(1)} %get-tuple-element.609), channel_id=1, source_target_pairs={{0,1},{1,2},{2,3},{3,4},{4,5},{5,6},{6,7},{7,8},{8,9},{9,10},{10,1... | collective-permute-start | bytes 786440 | tf_op jit(solution)/shard_map/while/body/eval_jaxpr/ppermute | solution.py:14
  120.3 0.7 copy-start
  121.0 9.8 %collective-permute-start = (f32[8,64,128]{2,1,0:T(8,128)S(1)}, f32[8,64,128]{2,1,0:T(8,128)S(1)}, u32[]{:S(2)}, u32[]{:S(2)}) collective-permute-start(f32[8,64,128]{2,1,0:T(8,128)S(1)} %get-tuple-element.609), channel_id=1, source_target_pairs={{0,1},{1,2},{2,3},{3,4},{4,5},{5,6},{6,7},{7,8},{8,9},{9,10},{10,1... | collective-permute-start | bytes 786440 | tf_op jit(solution)/shard_map/while/body/eval_jaxpr/ppermute | solution.py:14
  130.8 0.7 copy-start
  131.5 9.8 %collective-permute-start = (f32[8,64,128]{2,1,0:T(8,128)S(1)}, f32[8,64,128]{2,1,0:T(8,128)S(1)}, u32[]{:S(2)}, u32[]{:S(2)}) collective-permute-start(f32[8,64,128]{2,1,0:T(8,128)S(1)} %get-tuple-element.609), channel_id=1, source_target_pairs={{0,1},{1,2},{2,3},{3,4},{4,5},{5,6},{6,7},{7,8},{8,9},{9,10},{10,1... | collective-permute-start | bytes 786440 | tf_op jit(solution)/shard_map/while/body/eval_jaxpr/ppermute | solution.py:14
  142.0 9.8 %collective-permute-start = (f32[8,64,128]{2,1,0:T(8,128)S(1)}, f32[8,64,128]{2,1,0:T(8,128)S(1)}, u32[]{:S(2)}, u32[]{:S(2)}) collective-permute-start(f32[8,64,128]{2,1,0:T(8,128)S(1)} %get-tuple-element.609), channel_id=1, source_target_pairs={{0,1},{1,2},{2,3},{3,4},{4,5},{5,6},{6,7},{7,8},{8,9},{9,10},{10,1... | collective-permute-start | bytes 786440 | tf_op jit(solution)/shard_map/while/body/eval_jaxpr/ppermute | solution.py:14
  152.5 9.8 %collective-permute-start = (f32[8,64,128]{2,1,0:T(8,128)S(1)}, f32[8,64,128]{2,1,0:T(8,128)S(1)}, u32[]{:S(2)}, u32[]{:S(2)}) collective-permute-start(f32[8,64,128]{2,1,0:T(8,128)S(1)} %get-tuple-element.609), channel_id=1, source_target_pairs={{0,1},{1,2},{2,3},{3,4},{4,5},{5,6},{6,7},{7,8},{8,9},{9,10},{10,1... | collective-permute-start | bytes 786440 | tf_op jit(solution)/shard_map/while/body/eval_jaxpr/ppermute | solution.py:14
  163.0 9.8 %collective-permute-start = (f32[8,64,128]{2,1,0:T(8,128)S(1)}, f32[8,64,128]{2,1,0:T(8,128)S(1)}, u32[]{:S(2)}, u32[]{:S(2)}) collective-permute-start(f32[8,64,128]{2,1,0:T(8,128)S(1)} %get-tuple-element.609), channel_id=1, source_target_pairs={{0,1},{1,2},{2,3},{3,4},{4,5},{5,6},{6,7},{7,8},{8,9},{9,10},{10,1... | collective-permute-start | bytes 786440 | tf_op jit(solution)/shard_map/while/body/eval_jaxpr/ppermute | solution.py:14
  173.5 9.8 %collective-permute-start = (f32[8,64,128]{2,1,0:T(8,128)S(1)}, f32[8,64,128]{2,1,0:T(8,128)S(1)}, u32[]{:S(2)}, u32[]{:S(2)}) collective-permute-start(f32[8,64,128]{2,1,0:T(8,128)S(1)} %get-tuple-element.609), channel_id=1, source_target_pairs={{0,1},{1,2},{2,3},{3,4},{4,5},{5,6},{6,7},{7,8},{8,9},{9,10},{10,1... | collective-permute-start | bytes 786440 | tf_op jit(solution)/shard_map/while/body/eval_jaxpr/ppermute | solution.py:14
  184.0 9.8 %collective-permute-start = (f32[8,64,128]{2,1,0:T(8,128)S(1)}, f32[8,64,128]{2,1,0:T(8,128)S(1)}, u32[]{:S(2)}, u32[]{:S(2)}) collective-permute-start(f32[8,64,128]{2,1,0:T(8,128)S(1)} %get-tuple-element.609), channel_id=1, source_target_pairs={{0,1},{1,2},{2,3},{3,4},{4,5},{5,6},{6,7},{7,8},{8,9},{9,10},{10,1... | collective-permute-start | bytes 786440 | tf_op jit(solution)/shard_map/while/body/eval_jaxpr/ppermute | solution.py:14
  194.5 9.8 %collective-permute-start = (f32[8,64,128]{2,1,0:T(8,128)S(1)}, f32[8,64,128]{2,1,0:T(8,128)S(1)}, u32[]{:S(2)}, u32[]{:S(2)}) collective-permute-start(f32[8,64,128]{2,1,0:T(8,128)S(1)} %get-tuple-element.609), channel_id=1, source_target_pairs={{0,1},{1,2},{2,3},{3,4},{4,5},{5,6},{6,7},{7,8},{8,9},{9,10},{10,1... | collective-permute-start | bytes 786440 | tf_op jit(solution)/shard_map/while/body/eval_jaxpr/ppermute | solution.py:14
  205.0 9.8 %collective-permute-start = (f32[8,64,128]{2,1,0:T(8,128)S(1)}, f32[8,64,128]{2,1,0:T(8,128)S(1)}, u32[]{:S(2)}, u32[]{:S(2)}) collective-permute-start(f32[8,64,128]{2,1,0:T(8,128)S(1)} %get-tuple-element.609), channel_id=1, source_target_pairs={{0,1},{1,2},{2,3},{3,4},{4,5},{5,6},{6,7},{7,8},{8,9},{9,10},{10,1... | collective-permute-start | bytes 786440 | tf_op jit(solution)/shard_map/while/body/eval_jaxpr/ppermute | solution.py:14
  215.5 9.8 %collective-permute-start = (f32[8,64,128]{2,1,0:T(8,128)S(1)}, f32[8,64,128]{2,1,0:T(8,128)S(1)}, u32[]{:S(2)}, u32[]{:S(2)}) collective-permute-start(f32[8,64,128]{2,1,0:T(8,128)S(1)} %get-tuple-element.609), channel_id=1, source_target_pairs={{0,1},{1,2},{2,3},{3,4},{4,5},{5,6},{6,7},{7,8},{8,9},{9,10},{10,1... | collective-permute-start | bytes 786440 | tf_op jit(solution)/shard_map/while/body/eval_jaxpr/ppermute | solution.py:14
  225.9 9.8 %collective-permute-start = (f32[8,64,128]{2,1,0:T(8,128)S(1)}, f32[8,64,128]{2,1,0:T(8,128)S(1)}, u32[]{:S(2)}, u32[]{:S(2)}) collective-permute-start(f32[8,64,128]{2,1,0:T(8,128)S(1)} %get-tuple-element.609), channel_id=1, source_target_pairs={{0,1},{1,2},{2,3},{3,4},{4,5},{5,6},{6,7},{7,8},{8,9},{9,10},{10,1... | collective-permute-start | bytes 786440 | tf_op jit(solution)/shard_map/while/body/eval_jaxpr/ppermute | solution.py:14
  236.4 9.8 %collective-permute-start = (f32[8,64,128]{2,1,0:T(8,128)S(1)}, f32[8,64,128]{2,1,0:T(8,128)S(1)}, u32[]{:S(2)}, u32[]{:S(2)}) collective-permute-start(f32[8,64,128]{2,1,0:T(8,128)S(1)} %get-tuple-element.609), channel_id=1, source_target_pairs={{0,1},{1,2},{2,3},{3,4},{4,5},{5,6},{6,7},{7,8},{8,9},{9,10},{10,1... | collective-permute-start | bytes 786440 | tf_op jit(solution)/shard_map/while/body/eval_jaxpr/ppermute | solution.py:14
  246.9 9.8 %collective-permute-start = (f32[8,64,128]{2,1,0:T(8,128)S(1)}, f32[8,64,128]{2,1,0:T(8,128)S(1)}, u32[]{:S(2)}, u32[]{:S(2)}) collective-permute-start(f32[8,64,128]{2,1,0:T(8,128)S(1)} %get-tuple-element.609), channel_id=1, source_target_pairs={{0,1},{1,2},{2,3},{3,4},{4,5},{5,6},{6,7},{7,8},{8,9},{9,10},{10,1... | collective-permute-start | bytes 786440 | tf_op jit(solution)/shard_map/while/body/eval_jaxpr/ppermute | solution.py:14
  257.4 9.8 %collective-permute-start = (f32[8,64,128]{2,1,0:T(8,128)S(1)}, f32[8,64,128]{2,1,0:T(8,128)S(1)}, u32[]{:S(2)}, u32[]{:S(2)}) collective-permute-start(f32[8,64,128]{2,1,0:T(8,128)S(1)} %get-tuple-element.609), channel_id=1, source_target_pairs={{0,1},{1,2},{2,3},{3,4},{4,5},{5,6},{6,7},{7,8},{8,9},{9,10},{10,1... | collective-permute-start | bytes 786440 | tf_op jit(solution)/shard_map/while/body/eval_jaxpr/ppermute | solution.py:14
  267.9 9.8 %collective-permute-start = (f32[8,64,128]{2,1,0:T(8,128)S(1)}, f32[8,64,128]{2,1,0:T(8,128)S(1)}, u32[]{:S(2)}, u32[]{:S(2)}) collective-permute-start(f32[8,64,128]{2,1,0:T(8,128)S(1)} %get-tuple-element.609), channel_id=1, source_target_pairs={{0,1},{1,2},{2,3},{3,4},{4,5},{5,6},{6,7},{7,8},{8,9},{9,10},{10,1... | collective-permute-start | bytes 786440 | tf_op jit(solution)/shard_map/while/body/eval_jaxpr/ppermute | solution.py:14
  278.4 9.8 %collective-permute-start = (f32[8,64,128]{2,1,0:T(8,128)S(1)}, f32[8,64,128]{2,1,0:T(8,128)S(1)}, u32[]{:S(2)}, u32[]{:S(2)}) collective-permute-start(f32[8,64,128]{2,1,0:T(8,128)S(1)} %get-tuple-element.609), channel_id=1, source_target_pairs={{0,1},{1,2},{2,3},{3,4},{4,5},{5,6},{6,7},{7,8},{8,9},{9,10},{10,1... | collective-permute-start | bytes 786440 | tf_op jit(solution)/shard_map/while/body/eval_jaxpr/ppermute | solution.py:14
  288.2 0.7 copy-start
  288.9 9.8 %collective-permute-start = (f32[8,64,128]{2,1,0:T(8,128)S(1)}, f32[8,64,128]{2,1,0:T(8,128)S(1)}, u32[]{:S(2)}, u32[]{:S(2)}) collective-permute-start(f32[8,64,128]{2,1,0:T(8,128)S(1)} %get-tuple-element.609), channel_id=1, source_target_pairs={{0,1},{1,2},{2,3},{3,4},{4,5},{5,6},{6,7},{7,8},{8,9},{9,10},{10,1... | collective-permute-start | bytes 786440 | tf_op jit(solution)/shard_map/while/body/eval_jaxpr/ppermute | solution.py:14
  298.7 0.7 copy-start
  299.4 9.8 %collective-permute-start = (f32[8,64,128]{2,1,0:T(8,128)S(1)}, f32[8,64,128]{2,1,0:T(8,128)S(1)}, u32[]{:S(2)}, u32[]{:S(2)}) collective-permute-start(f32[8,64,128]{2,1,0:T(8,128)S(1)} %get-tuple-element.609), channel_id=1, source_target_pairs={{0,1},{1,2},{2,3},{3,4},{4,5},{5,6},{6,7},{7,8},{8,9},{9,10},{10,1... | collective-permute-start | bytes 786440 | tf_op jit(solution)/shard_map/while/body/eval_jaxpr/ppermute | solution.py:14
  309.2 0.7 copy-start
  309.9 9.8 %collective-permute-start = (f32[8,64,128]{2,1,0:T(8,128)S(1)}, f32[8,64,128]{2,1,0:T(8,128)S(1)}, u32[]{:S(2)}, u32[]{:S(2)}) collective-permute-start(f32[8,64,128]{2,1,0:T(8,128)S(1)} %get-tuple-element.609), channel_id=1, source_target_pairs={{0,1},{1,2},{2,3},{3,4},{4,5},{5,6},{6,7},{7,8},{8,9},{9,10},{10,1... | collective-permute-start | bytes 786440 | tf_op jit(solution)/shard_map/while/body/eval_jaxpr/ppermute | solution.py:14
  319.7 0.7 copy-start
  320.4 9.8 %collective-permute-start = (f32[8,64,128]{2,1,0:T(8,128)S(1)}, f32[8,64,128]{2,1,0:T(8,128)S(1)}, u32[]{:S(2)}, u32[]{:S(2)}) collective-permute-start(f32[8,64,128]{2,1,0:T(8,128)S(1)} %get-tuple-element.609), channel_id=1, source_target_pairs={{0,1},{1,2},{2,3},{3,4},{4,5},{5,6},{6,7},{7,8},{8,9},{9,10},{10,1... | collective-permute-start | bytes 786440 | tf_op jit(solution)/shard_map/while/body/eval_jaxpr/ppermute | solution.py:14
  330.2 0.7 copy-start
  330.9 9.8 %collective-permute-start = (f32[8,64,128]{2,1,0:T(8,128)S(1)}, f32[8,64,128]{2,1,0:T(8,128)S(1)}, u32[]{:S(2)}, u32[]{:S(2)}) collective-permute-start(f32[8,64,128]{2,1,0:T(8,128)S(1)} %get-tuple-element.609), channel_id=1, source_target_pairs={{0,1},{1,2},{2,3},{3,4},{4,5},{5,6},{6,7},{7,8},{8,9},{9,10},{10,1... | collective-permute-start | bytes 786440 | tf_op jit(solution)/shard_map/while/body/eval_jaxpr/ppermute | solution.py:14
  341.4 9.8 %collective-permute-start = (f32[8,64,128]{2,1,0:T(8,128)S(1)}, f32[8,64,128]{2,1,0:T(8,128)S(1)}, u32[]{:S(2)}, u32[]{:S(2)}) collective-permute-start(f32[8,64,128]{2,1,0:T(8,128)S(1)} %get-tuple-element.609), channel_id=1, source_target_pairs={{0,1},{1,2},{2,3},{3,4},{4,5},{5,6},{6,7},{7,8},{8,9},{9,10},{10,1... | collective-permute-start | bytes 786440 | tf_op jit(solution)/shard_map/while/body/eval_jaxpr/ppermute | solution.py:14
  351.8 9.8 %collective-permute-start = (f32[8,64,128]{2,1,0:T(8,128)S(1)}, f32[8,64,128]{2,1,0:T(8,128)S(1)}, u32[]{:S(2)}, u32[]{:S(2)}) collective-permute-start(f32[8,64,128]{2,1,0:T(8,128)S(1)} %get-tuple-element.609), channel_id=1, source_target_pairs={{0,1},{1,2},{2,3},{3,4},{4,5},{5,6},{6,7},{7,8},{8,9},{9,10},{10,1... | collective-permute-start | bytes 786440 | tf_op jit(solution)/shard_map/while/body/eval_jaxpr/ppermute | solution.py:14
  365.2 3.2 copy-start.3
  374.5 37.4 %copy-start.2 = (f32[512]{0:T(512)S(1)}, f32[512]{0:T(512)}, u32[]{:S(2)}) copy-start(f32[512]{0:T(512)} %param.23) | copy-start | bytes 6148
  (17 other events, 11.9 us)
where the time goes:
time: 417 us; the launch traced here: 416 us
  waiting for transfers between devices  244 us (59%)
  starting transfers between devices  59.2 us (14%)
  local copies, waits for them, and re-layouts  38.4 us (9%)
  blocking collectives  36.5 us (9%)
  other arithmetic  19.1 us (5%)
  matrix products  14.7 us (4%)
    ppermute x31, waiting for transfers between devices, from_behind(): return lax.ppermute(block, axis, route)  244 us
    ppermute x31, starting transfers between devices, from_behind(): return lax.ppermute(block, axis, route)  59.2 us
    psum x1, blocking collectives, on_device(): total_squares = lax.psum(partial_squares, 'head')  36.5 us
    while x62, local copies, waits for them, and re-layouts  18.8 us
  transfers between devices with their start and end apart: 31, of which 31 were waited for; matrix products, arithmetic and copies ran while one was open for 0% of the time, Pallas kernels for 0%

commit v1 on v0

v1 whole, which is shorter than its diff:
```python
import functools

import jax
import jax.numpy as jnp
from jax import lax
from jax.experimental import pallas as pl
from jax.experimental.pallas import tpu as pltpu
from jax.sharding import PartitionSpec as P

MESH = pl.DeviceIdType.MESH
CHUNK = 128
HALF = CHUNK // 2
ROWS = 8
EPS = 1e-05
TO_END, TO_KEY, TO_QUERY, FROM_CHUNK, FROM_DEVICE = range(5)
KINDS = 5
REQUEST_ROW = KINDS * ROWS
F32, BF16 = jnp.float32, jnp.bfloat16


def iota(shape, dim):
    return lax.broadcasted_iota(jnp.int32, shape, dim)


def matmul(left, right):
    return jnp.dot(left, right, preferred_element_type=F32)


def kernel(
    nh, nc, group_heads, lengths, skip, x_hbm, z_hbm, b_hbm, c_hbm, decay_hbm, gain_hbm, out_hbm,
    x, z, b, c, decay, gain, out, table, spread, spread_request, requests, local_state, state,
    partial, gate, decay_out, decay_in, slice_out, slice_in, enter_out, enter_in, square_out, square_in,
    load_sem, store_sem, send_sem, recv_sem,
):
    head_pos = lax.axis_index("head")
    ctx_pos = lax.axis_index("ctx")
    tokens, lanes = x.shape
    chunks = tokens // CHUNK
    width = lanes // ROWS
    state_size = b.shape[1]
    share = slice_in.shape[2]
    share_rows = slice_in.shape[1]
    group = head_pos * ROWS // group_heads
    columns = pl.ds(pl.multiple_of(group * state_size, state_size), state_size)
    loads = [
        pltpu.make_async_copy(decay_hbm, decay, load_sem.at[0]),
        pltpu.make_async_copy(x_hbm, x, load_sem.at[1]),
        pltpu.make_async_copy(b_hbm.at[:, columns], b, load_sem.at[2]),
        pltpu.make_async_copy(c_hbm.at[:, columns], c, load_sem.at[3]),
        pltpu.make_async_copy(z_hbm, z, load_sem.at[4]),
        pltpu.make_async_copy(gain_hbm, gain, load_sem.at[5]),
    ]
    for load in loads:
        load.start()

    barrier = pltpu.get_barrier_semaphore()

    def greet(axis, place, count):
        def one(step, carry):
            pl.semaphore_signal(
                barrier, inc=1, device_id={axis: lax.rem(place + step, count)}, device_id_type=MESH
            )
            return carry

        lax.fori_loop(1, count, one, 0)

    greet("ctx", ctx_pos, nc)
    greet("head", head_pos, nh)

    def exchange(axis, place, count, source, target, which):
        def one(step, carry):
            other = lax.rem(place + step, count)
            pltpu.make_async_remote_copy(
                src_ref=source(other),
                dst_ref=target.at[place],
                send_sem=send_sem.at[which],
                recv_sem=recv_sem.at[which],
                device_id={axis: other},
                device_id_type=MESH,
            ).start()
            return carry

        lax.fori_loop(1, count, one, 0)

    def arrival(axis, place, count, target, which):
        return pltpu.make_async_remote_copy(
            src_ref=target.at[pl.ds(0, count - 1)],
            dst_ref=target.at[pl.ds(0, count - 1)],
            send_sem=send_sem.at[which],
            recv_sem=recv_sem.at[which],
            device_id={axis: lax.rem(place + 1, count)},
            device_id_type=MESH,
        )

    starts = []
    running = jnp.int32(0)
    for r in range(lengths.shape[0]):
        starts.append(running)
        running = running + lengths[r]

    def request_at(position):
        total = jnp.zeros(position.shape, F32)
        for start in starts:
            total = total + jnp.where(position >= start, 1.0, 0.0)
        return total

    chunk_first = ctx_pos * tokens + iota((chunks, CHUNK), 0) * CHUNK
    request = request_at(chunk_first + iota((chunks, CHUNK), 1))
    request_end = request_at(chunk_first + (CHUNK - 1))
    request_prior = request_at(chunk_first - 1)
    live_end = jnp.where(request == request_end, 1.0, 0.0)
    live_start = jnp.where(request == request_prior, 1.0, 0.0)
    requests[...] = request

    row = iota((CHUNK, lanes), 0)
    row = jnp.where(row >= HALF, row - HALF, row)
    head_of_lane = iota((CHUNK, lanes), 1) // width
    for kind in range(KINDS):
        spread[kind] = jnp.where(row == kind * ROWS + head_of_lane, 1.0, 0.0).astype(BF16)
    spread_request[...] = jnp.where(iota((CHUNK, CHUNK), 0) == REQUEST_ROW, 1.0, 0.0).astype(BF16)
    lane_head = iota((1, lanes), 1) // width
    skip_row = jnp.zeros((1, lanes), F32)
    for h in range(ROWS):
        skip_row = jnp.where(lane_head == h, skip[h], skip_row)

    loads[0].wait()
    upper = jnp.where(iota((CHUNK, CHUNK), 0) <= iota((CHUNK, CHUNK), 1), 1.0, 0.0)
    stacked = jnp.concatenate([decay[:, k * CHUNK : (k + 1) * CHUNK] for k in range(chunks)], axis=0)
    cum = jnp.dot(stacked, upper, preferred_element_type=F32, precision=lax.Precision.HIGHEST)
    before = jnp.ones((ROWS, CHUNK), F32)
    for k in range(chunks):
        part = cum[k * ROWS : (k + 1) * ROWS]
        middle = jnp.broadcast_to(part[:, HALF - 1 : HALF], part.shape)
        end = jnp.broadcast_to(part[:, CHUNK - 1 :], part.shape)
        from_start = jnp.exp(part) * live_start[k : k + 1]
        factors = [
            jnp.exp(end - part) * live_end[k : k + 1],
            jnp.exp(middle - part),
            jnp.exp(part - middle),
            from_start,
            from_start * before,
        ]
        before = before * jnp.broadcast_to(from_start[:, CHUNK - 1 :], part.shape)
        values = jnp.concatenate(factors, axis=0)
        high = values.astype(BF16).astype(F32)
        request_rows = jnp.broadcast_to(request[k : k + 1], (ROWS, CHUNK))
        blank = jnp.zeros((HALF - REQUEST_ROW - ROWS, CHUNK), F32)
        blank_low = jnp.zeros((HALF - REQUEST_ROW, CHUNK), F32)
        whole = jnp.concatenate([high, request_rows, blank, values - high, blank_low], axis=0)
        table[k] = whole.T.astype(BF16)

    def last_row(k, kind):
        return matmul(table[k, CHUNK - 16 :, :], spread[kind])[15:16]

    decay_out[...] = last_row(chunks - 1, FROM_DEVICE)

    loads[1].wait()
    loads[2].wait()
    state[...] = jnp.zeros(state.shape, F32)

    def at(k):
        return pl.ds(pl.multiple_of(k * CHUNK, CHUNK), CHUNK)

    def add_state(k, carry):
        local_state[k] = state[...].astype(BF16)
        scaled = (x[at(k), :].astype(F32) * matmul(table[k], spread[TO_END])).astype(BF16)
        added = lax.dot_general(
            b[at(k), :], scaled, (((0,), (0,)), ((), ())), preferred_element_type=F32
        )
        state[...] = last_row(k, FROM_CHUNK) * state[...] + added
        return carry

    lax.fori_loop(0, chunks, add_state, 0)
    halves = lanes // share
    for i in range(nc):
        top, left = (i // halves) * share_rows, (i % halves) * share
        slice_out[i] = state[top : top + share_rows, left : left + share]

    pl.semaphore_wait(barrier, nc - 1 + nh - 1)
    exchange("ctx", ctx_pos, nc, lambda other: decay_out, decay_in, 0)
    exchange("ctx", ctx_pos, nc, lambda other: slice_out.at[other], slice_in, 1)
    decay_in[ctx_pos] = decay_out[...]
    slice_in[ctx_pos] = slice_out[ctx_pos]

    loads[3].wait()
    loads[4].wait()
    causal = iota((CHUNK, CHUNK), 0) >= iota((CHUNK, CHUNK), 1)

    def own_part(k, carry):
        rows = at(k)
        maps = c[rows, :]
        scores = lax.dot_general(
            maps, b[rows, :], (((1,), (1,)), ((), ())), preferred_element_type=F32
        )
        same = matmul(table[k], spread_request[...]) == requests[pl.ds(k, 1), :]
        scores = jnp.where(causal & same, scores, 0.0).astype(BF16)
        wide = x[rows, :].astype(F32)
        keys = (wide * matmul(table[k], spread[TO_KEY])).astype(BF16)
        total = matmul(scores, keys) * matmul(table[k], spread[TO_QUERY])
        total += matmul(maps, local_state[k]) * matmul(table[k], spread[FROM_CHUNK])
        partial[rows, :] = total + skip_row * wide
        branch = z[rows, :].astype(F32)
        gate[rows, :] = branch / (1.0 + jnp.exp(-branch))
        return carry

    lax.fori_loop(0, chunks, own_part, 0)

    for target, which in ((decay_in, 0), (slice_in, 1)):
        arrived = arrival("ctx", ctx_pos, nc, target, which)
        arrived.wait_recv()
        arrived.wait_send()
    side = pl.ds(pl.multiple_of(lax.rem(ctx_pos, halves) * share, share), share)

    def scan(i, entering):
        enter_out[i] = entering
        return decay_in[i, :, side] * entering + slice_in[i]

    lax.fori_loop(0, nc, scan, jnp.zeros((share_rows, share), F32))
    exchange("ctx", ctx_pos, nc, lambda other: enter_out.at[other], enter_in, 2)
    enter_in[ctx_pos] = enter_out[ctx_pos]
    arrived = arrival("ctx", ctx_pos, nc, enter_in, 2)
    arrived.wait_recv()
    for i in range(nc):
        top, left = (i // halves) * share_rows, (i % halves) * share
        state[top : top + share_rows, left : left + share] = enter_in[i]
    local_state[0] = state[...].astype(BF16)

    def add_carried(k, carry):
        rows = at(k)
        carried = matmul(c[rows, :], local_state[0]) * matmul(table[k], spread[FROM_DEVICE])
        output = (partial[rows, :] + carried).astype(BF16).astype(F32)
        gated = output * gate[rows, :]
        partial[rows, :] = gated
        squared = gated * gated
        folded = squared[:, :CHUNK]
        for i in range(1, lanes // CHUNK):
            folded = folded + squared[:, i * CHUNK : (i + 1) * CHUNK]
        square_out[pl.ds(k, 1), :] = jnp.sum(folded.T, axis=0, keepdims=True)
        return carry

    lax.fori_loop(0, chunks, add_carried, 0)
    arrived.wait_send()

    exchange("head", head_pos, nh, lambda other: square_out, square_in, 3)
    square_in[head_pos] = square_out[...]
    loads[5].wait()
    arrived = arrival("head", head_pos, nh, square_in, 3)
    arrived.wait_recv()
    squares = square_in[0]
    for i in range(1, nh):
        squares = squares + square_in[i]
    requests[...] = lax.rsqrt(squares / (nh * lanes) + EPS)

    def normalize(k, carry):
        rows = at(k)
        scale = jnp.broadcast_to(requests[pl.ds(k, 1), :], (CHUNK, CHUNK)).T
        scale = jnp.concatenate([scale] * (lanes // CHUNK), axis=1)
        out[rows, :] = (partial[rows, :] * scale * gain[...]).astype(BF16)
        pltpu.make_async_copy(out.at[rows, :], out_hbm.at[rows, :], store_sem).start()
        return carry

    lax.fori_loop(0, chunks, normalize, 0)
    arrived.wait_send()
    pltpu.make_async_copy(out, out_hbm, store_sem).wait()


def on_device(nh, nc, head_inputs, gate_z, input_b, output_c, log_decay, lengths, skip_coef, norm_gain):
    tokens, lanes = head_inputs.shape
    heads = skip_coef.shape[0]
    assert heads == ROWS and tokens == ROWS * CHUNK
    state_size = CHUNK
    groups = input_b.shape[1] // state_size
    chunks = tokens // CHUNK
    share = lanes // 2
    share_rows = 2 * state_size // nc
    vmem, smem, anywhere = pltpu.VMEM, pltpu.SMEM, pl.ANY
    return pl.pallas_call(
        functools.partial(kernel, nh, nc, heads * nh // groups),
        out_shape=jax.ShapeDtypeStruct((tokens, lanes), BF16),
        in_specs=[pl.BlockSpec(memory_space=smem)] * 2 + [pl.BlockSpec(memory_space=anywhere)] * 6,
        out_specs=pl.BlockSpec(memory_space=anywhere),
        scratch_shapes=[
            vmem((tokens, lanes), BF16),
            vmem((tokens, lanes), BF16),
            vmem((tokens, state_size), BF16),
            vmem((tokens, state_size), BF16),
            vmem((heads, tokens), F32),
            vmem((1, lanes), F32),
            vmem((tokens, lanes), BF16),
            vmem((chunks, CHUNK, CHUNK), BF16),
            vmem((KINDS, CHUNK, lanes), BF16),
            vmem((CHUNK, CHUNK), BF16),
            vmem((chunks, CHUNK), F32),
            vmem((chunks, state_size, lanes), BF16),
            vmem((state_size, lanes), F32),
            vmem((tokens, lanes), F32),
            vmem((tokens, lanes), F32),
            vmem((1, lanes), F32),
            vmem((nc, 1, lanes), F32),
            vmem((nc, share_rows, share), F32),
            vmem((nc, share_rows, share), F32),
            vmem((nc, share_rows, share), F32),
            vmem((nc, share_rows, share), F32),
            vmem((chunks, CHUNK), F32),
            vmem((nh, chunks, CHUNK), F32),
            pltpu.SemaphoreType.DMA((6,)),
            pltpu.SemaphoreType.DMA,
            pltpu.SemaphoreType.DMA((4,)),
            pltpu.SemaphoreType.DMA((4,)),
        ],
        compiler_params=pltpu.CompilerParams(collective_id=0, has_side_effects=True),
    )(
        lengths, skip_coef, head_inputs, gate_z, input_b, output_c, log_decay.T,
        norm_gain.reshape(1, lanes),
    )


def solution(mesh):
    return jax.shard_map(
        functools.partial(on_device, mesh.shape["head"], mesh.shape["ctx"]),
        mesh=mesh,
        in_specs=(
            P("ctx", "head"),
            P("ctx", "head"),
            P("ctx", None),
            P("ctx", None),
            P("ctx", "head"),
            P(),
            P("head"),
            P("head"),
        ),
        out_specs=P("ctx", "head"),
        check_vma=False,
    )
```

time: 417 us -> 43.6 us (0.10)
  the two profiles are of different devices: /device:TPU:6 before, /device:TPU:1 now
where the time goes in v1:
time: 43.6 us; the launch traced here: 43.4 us
  Pallas kernels  41.2 us (94%)
  local copies, waits for them, and re-layouts  2.26 us (5%)
    pallas_call x1, Pallas kernels, on_device(): pl.pallas_call(functools.partial(kernel, nh, nc, heads * nh // groups), o...  41.2 us
    unnamed x1, local copies, waits for them, and re-layouts  2.26 us

profile of v1, /device:TPU:1, one launch (start us, length us, event | category | flops | bytes accessed | tf_op | source)
XLA Modules:
  0.0 43.4 jit_solution(8992262886999827344)
XLA Ops:
  0.0 41.2 %shard_map.82 = bf16[1024,512]{1,0:T(8,128)(2,1)} custom-call(s32[16]{0:T(128)} %lengths.1, f32[8]{0:T(128)} %skip.1, bf16[1024,512]{1,0:T(8,128)(2,1)} %x_hbm.1, bf16[1024,512]{1,0:T(8,128)(2,1)} %z_hbm.1, bf16[1024,1024]{1,0:T(8,128)(2,1)} %b_hbm.1, bf16[1024,1024]{1,0:T(8,128)(2,1)} %c_hbm.1, f32[8,1024]{1,0:T(8,128)} %bitcast.2, f32[1,512]{1,0:T(1,128)} %bitcast.3), custom_call_target="tpu_custom_call" | custom-call | tf_op jit(solution)/shard_map/pallas_call | solution.py:277
  41.2 2.3 %copy.10 = bf16[1024,512]{1,0:T(8,128)(2,1)} copy(bf16[1024,512]{1,0:T(8,128)(2,1)} %shard_map.82) | data formatting | bytes 2097152

commit v2 on v1

v2 whole, which is shorter than its diff:
```python
import functools
import math

import jax
import jax.numpy as jnp
from jax import lax
from jax.experimental import pallas as pl
from jax.experimental.pallas import tpu as pltpu
from jax.sharding import PartitionSpec as P

MESH = pl.DeviceIdType.MESH
CHUNK = 128
HALF = CHUNK // 2
ROWS = 8
EPS = 1e-05
TO_END, TO_KEY, TO_QUERY, FROM_CHUNK, FROM_DEVICE = range(5)
KINDS = 5
REQUEST_ROW = KINDS * ROWS
F32, BF16 = jnp.float32, jnp.bfloat16


def iota(shape, dim):
    return lax.broadcasted_iota(jnp.int32, shape, dim)


def matmul(left, right):
    return jnp.dot(left, right, preferred_element_type=F32)


def around(offset, count):
    return min(offset, count - offset)


def kernel(
    nh, nc, group_heads, lengths_hbm, skip_hbm, x_hbm, z_hbm, b_hbm, c_hbm, decay_hbm, gated, scales,
    lengths, skip, x, z, b, c, b_turned, decay, table, spread, spread_request, requests, leaving, local_state, state,
    partial, gate, from_device, decay_out, decay_in, slice_out, slice_in, enter_out, enter_in,
    square_out, square_in, load_sem, send_sem, recv_sem,
):
    head_pos = lax.axis_index("head")
    ctx_pos = lax.axis_index("ctx")
    tokens, lanes = x.shape
    chunks = tokens // CHUNK
    width = lanes // ROWS
    state_size = b.shape[1]
    share_rows, share = slice_in.shape[1:]
    group = head_pos * ROWS // group_heads
    columns = pl.ds(pl.multiple_of(group * state_size, state_size), state_size)
    loads = [
        pltpu.make_async_copy(decay_hbm, decay, load_sem.at[0]),
        pltpu.make_async_copy(b_hbm.at[:, columns], b, load_sem.at[1]),
        pltpu.make_async_copy(x_hbm, x, load_sem.at[2]),
        pltpu.make_async_copy(c_hbm.at[:, columns], c, load_sem.at[3]),
        pltpu.make_async_copy(z_hbm, z, load_sem.at[4]),
        pltpu.make_async_copy(skip_hbm, skip, load_sem.at[5]),
        pltpu.make_async_copy(lengths_hbm, lengths, load_sem.at[6]),
    ]
    for i in (6, 0, 1, 2, 3, 4, 5):
        loads[i].start()

    barrier = pltpu.get_barrier_semaphore()

    def greet(axis, place, count):
        def one(step, carry):
            pl.semaphore_signal(
                barrier, inc=1, device_id={axis: lax.rem(place + step, count)}, device_id_type=MESH
            )
            return carry

        lax.fori_loop(1, count, one, 0)

    greet("ctx", ctx_pos, nc)
    greet("head", head_pos, nh)

    def send(axis, place, other, source, target, which):
        pltpu.make_async_remote_copy(
            src_ref=source,
            dst_ref=target.at[place],
            send_sem=send_sem.at[which],
            recv_sem=recv_sem.at[which],
            device_id={axis: other},
            device_id_type=MESH,
        ).start()

    side = math.isqrt(nc // 2)
    core = lax.rem(ctx_pos, 2)
    chip_row, chip_column = ctx_pos // (2 * side), lax.rem(ctx_pos // 2, side)
    hops = sorted(
        ((i, j) for i in range(side) for j in range(side)),
        key=lambda hop: -around(hop[0], side) - around(hop[1], side),
    )

    def send_to_core(which_core, source, target, which):
        for down, along in hops:
            chip = lax.rem(chip_row + down, side) * side + lax.rem(chip_column + along, side)
            other = 2 * chip + which_core
            if (down, along) == (0, 0):

                @pl.when(core != which_core)
                def _():
                    send("ctx", ctx_pos, other, source(other), target, which)

            else:
                send("ctx", ctx_pos, other, source(other), target, which)

    def arrival(axis, place, count, target, which):
        return pltpu.make_async_remote_copy(
            src_ref=target.at[pl.ds(0, count - 1)],
            dst_ref=target.at[pl.ds(0, count - 1)],
            send_sem=send_sem.at[which],
            recv_sem=recv_sem.at[which],
            device_id={axis: lax.rem(place + 1, count)},
            device_id_type=MESH,
        )

    loads[6].wait()
    starts = []
    running = jnp.int32(0)
    for r in range(lengths.shape[0]):
        starts.append(running)
        running = running + lengths[r]

    def request_at(position):
        total = jnp.zeros(position.shape, F32)
        for start in starts:
            total = total + jnp.where(position >= start, 1.0, 0.0)
        return total

    chunk_first = ctx_pos * tokens + iota((chunks, CHUNK), 0) * CHUNK
    request = request_at(chunk_first + iota((chunks, CHUNK), 1))
    request_end = request_at(chunk_first + (CHUNK - 1))
    request_prior = request_at(chunk_first - 1)
    live_end = jnp.where(request == request_end, 1.0, 0.0)
    live_start = jnp.where(request == request_prior, 1.0, 0.0)
    requests[...] = request

    row = iota((CHUNK, lanes), 0)
    row = jnp.where(row >= HALF, row - HALF, row)
    head_of_lane = iota((CHUNK, lanes), 1) // width
    for kind in range(KINDS):
        spread[kind] = jnp.where(row == kind * ROWS + head_of_lane, 1.0, 0.0).astype(BF16)
    spread_request[...] = jnp.where(iota((CHUNK, CHUNK), 0) == REQUEST_ROW, 1.0, 0.0).astype(BF16)

    loads[0].wait()
    upper = jnp.where(iota((CHUNK, CHUNK), 0) <= iota((CHUNK, CHUNK), 1), 1.0, 0.0)
    stacked = jnp.concatenate([decay[:, k * CHUNK : (k + 1) * CHUNK] for k in range(chunks)], axis=0)
    cum = jnp.dot(stacked, upper, preferred_element_type=F32, precision=lax.Precision.HIGHEST)
    before = jnp.ones((ROWS, CHUNK), F32)
    for k in range(chunks):
        part = cum[k * ROWS : (k + 1) * ROWS]
        middle = jnp.broadcast_to(part[:, HALF - 1 : HALF], part.shape)
        end = jnp.broadcast_to(part[:, CHUNK - 1 :], part.shape)
        from_start = jnp.exp(part) * live_start[k : k + 1]
        factors = [
            jnp.exp(end - part) * live_end[k : k + 1],
            jnp.exp(middle - part),
            jnp.exp(part - middle),
            from_start,
            from_start * before,
        ]
        before = before * jnp.broadcast_to(from_start[:, CHUNK - 1 :], part.shape)
        values = jnp.concatenate(factors, axis=0)
        high = values.astype(BF16).astype(F32)
        request_rows = jnp.broadcast_to(request[k : k + 1], (ROWS, CHUNK))
        blank = jnp.zeros((HALF - REQUEST_ROW - ROWS, CHUNK), F32)
        blank_low = jnp.zeros((HALF - REQUEST_ROW, CHUNK), F32)
        whole = jnp.concatenate([high, request_rows, blank, values - high, blank_low], axis=0)
        table[k] = whole.T.astype(BF16)
    decay_out[...] = table[chunks - 1, CHUNK - 16 :, :].astype(F32)[15:16]
    leaving[...] = matmul(table[:, CHUNK - 16 :, :].reshape(16 * chunks, CHUNK), spread[FROM_CHUNK])

    loads[1].wait()
    for k in range(chunks):
        b_turned[k] = b[k * CHUNK : (k + 1) * CHUNK, :].T
    loads[2].wait()
    for half in range(2):
        part = slice(half * share, (half + 1) * share)
        entering = jnp.zeros((state_size, share), F32)
        for k in range(chunks):
            rows = slice(k * CHUNK, (k + 1) * CHUNK)
            local_state[k, :, part] = entering.astype(BF16)
            scaled = (x[rows, part].astype(F32) * matmul(table[k], spread[TO_END, :, part])).astype(BF16)
            entering = leaving[16 * k + 15 : 16 * k + 16, part] * entering + matmul(b_turned[k], scaled)
        for i in range(nc // 2):
            slice_out[2 * i + half] = entering[i * share_rows : (i + 1) * share_rows]
        if half == 0:
            pl.semaphore_wait(barrier, nc - 1 + nh - 1)
            for which_core in range(2):
                send_to_core(which_core, lambda other: decay_out, decay_in, 0)
        send_to_core(half, lambda other: slice_out.at[other], slice_in, 1)
    decay_in[ctx_pos] = decay_out[...]
    slice_in[ctx_pos] = slice_out[ctx_pos]

    def at(k):
        return pl.ds(pl.multiple_of(k * CHUNK, CHUNK), CHUNK)

    loads[3].wait()
    loads[4].wait()
    loads[5].wait()
    lane_head = iota((1, lanes), 1) // width
    skip_row = jnp.zeros((1, lanes), F32)
    for h in range(ROWS):
        skip_row = jnp.where(lane_head == h, skip[h], skip_row)
    causal = iota((CHUNK, CHUNK), 0) >= iota((CHUNK, CHUNK), 1)

    def own_part(k, carry):
        rows = at(k)
        maps = c[rows, :]
        same = matmul(table[k], spread_request[...]) == requests[pl.ds(k, 1), :]
        scores = jnp.where(causal & same, matmul(maps, b_turned[k]), 0.0).astype(BF16)
        wide = x[rows, :].astype(F32)
        keys = (wide * matmul(table[k], spread[TO_KEY])).astype(BF16)
        total = matmul(scores, keys) * matmul(table[k], spread[TO_QUERY])
        total += matmul(maps, local_state[k]) * matmul(table[k], spread[FROM_CHUNK])
        partial[rows, :] = total + skip_row * wide
        from_device[rows, :] = matmul(table[k], spread[FROM_DEVICE])
        branch = z[rows, :].astype(F32)
        gate[rows, :] = branch / (1.0 + jnp.exp(-branch))
        return carry

    lax.fori_loop(0, chunks, own_part, 0)

    for target, which in ((decay_in, 0), (slice_in, 1)):
        arrived = arrival("ctx", ctx_pos, nc, target, which)
        arrived.wait_recv()
        arrived.wait_send()
    rows_in = jnp.concatenate([decay_in[i] for i in range(nc)], axis=0).astype(BF16)
    part = pl.ds(pl.multiple_of(core * share, share), share)
    steps = matmul(rows_in, spread[FROM_DEVICE, :, part])
    entering = jnp.zeros((share_rows, share), F32)
    for i in range(nc):
        enter_out[i] = entering
        entering = steps[i : i + 1] * entering + slice_in[i]
    for which_core in range(2):
        send_to_core(which_core, lambda other: enter_out.at[other], enter_in, 2)
    enter_in[ctx_pos] = enter_out[ctx_pos]
    arrived = arrival("ctx", ctx_pos, nc, enter_in, 2)
    arrived.wait_recv()
    for half in range(2):
        for i in range(nc // 2):
            state[i * share_rows : (i + 1) * share_rows, half * share : (half + 1) * share] = enter_in[2 * i + half]
    entered = state[...].astype(BF16)

    step_rows = 2 * CHUNK
    for k in range(tokens // step_rows):
        rows = slice(k * step_rows, (k + 1) * step_rows)
        output = partial[rows, :] + matmul(c[rows, :], entered) * from_device[rows, :]
        gates = output.astype(BF16).astype(F32) * gate[rows, :]
        gated[rows, :] = gates
        squared = gates * gates
        folded = squared[:, :CHUNK]
        for i in range(1, lanes // CHUNK):
            folded = folded + squared[:, i * CHUNK : (i + 1) * CHUNK]
        for i in range(2):
            square_out[2 * k + i : 2 * k + i + 1, :] = jnp.sum(
                folded[i * CHUNK : (i + 1) * CHUNK].T, axis=0, keepdims=True
            )

    for offset in sorted(range(1, nh), key=lambda offset: -around(offset, nh)):
        send("head", head_pos, lax.rem(head_pos + offset, nh), square_out, square_in, 3)
    square_in[head_pos] = square_out[...]
    arrived.wait_send()
    arrived = arrival("head", head_pos, nh, square_in, 3)
    arrived.wait_recv()
    squares = square_in[0]
    for i in range(1, nh):
        squares = squares + square_in[i]
    scales[...] = lax.rsqrt(squares / (nh * lanes) + EPS)
    arrived.wait_send()


def normalize(gated, scales, gain, out_hbm, out, sem):
    tokens, lanes = gated.shape
    copies = []
    for k in range(tokens // CHUNK):
        rows = slice(k * CHUNK, (k + 1) * CHUNK)
        scale = jnp.broadcast_to(scales[k : k + 1, :], (CHUNK, CHUNK)).T
        scale = jnp.concatenate([scale] * (lanes // CHUNK), axis=1)
        out[rows, :] = (gated[rows, :] * scale * gain[...]).astype(BF16)
        copies.append(pltpu.make_async_copy(out.at[rows, :], out_hbm.at[rows, :], sem.at[k]))
        copies[-1].start()
    for copy in copies:
        copy.wait()


def on_device(nh, nc, head_inputs, gate_z, input_b, output_c, log_decay, lengths, skip_coef, norm_gain):
    tokens, lanes = head_inputs.shape
    heads = skip_coef.shape[0]
    assert heads == ROWS and tokens == ROWS * CHUNK
    state_size = CHUNK
    groups = input_b.shape[1] // state_size
    chunks = tokens // CHUNK
    share = lanes // 2
    share_rows = 2 * state_size // nc
    vmem, smem, hbm = pltpu.VMEM, pltpu.SMEM, pltpu.HBM
    gated, scales = pl.pallas_call(
        functools.partial(kernel, nh, nc, heads * nh // groups),
        out_shape=(
            jax.ShapeDtypeStruct((tokens, lanes), F32),
            jax.ShapeDtypeStruct((chunks, CHUNK), F32),
        ),
        in_specs=[pl.BlockSpec(memory_space=hbm)] * 7,
        out_specs=(pl.BlockSpec(memory_space=vmem), pl.BlockSpec(memory_space=vmem)),
        scratch_shapes=[
            smem(lengths.shape, jnp.int32),
            smem(skip_coef.shape, F32),
            vmem((tokens, lanes), BF16),
            vmem((tokens, lanes), BF16),
            vmem((tokens, state_size), BF16),
            vmem((tokens, state_size), BF16),
            vmem((chunks, state_size, CHUNK), BF16),
            vmem((heads, tokens), F32),
            vmem((chunks, CHUNK, CHUNK), BF16),
            vmem((KINDS, CHUNK, lanes), BF16),
            vmem((CHUNK, CHUNK), BF16),
            vmem((chunks, CHUNK), F32),
            vmem((16 * chunks, lanes), F32),
            vmem((chunks, state_size, lanes), BF16),
            vmem((state_size, lanes), F32),
            vmem((tokens, lanes), F32),
            vmem((tokens, lanes), F32),
            vmem((tokens, lanes), F32),
            vmem((1, CHUNK), F32),
            vmem((nc, 1, CHUNK), F32),
            vmem((nc, share_rows, share), F32),
            vmem((nc, share_rows, share), F32),
            vmem((nc, share_rows, share), F32),
            vmem((nc, share_rows, share), F32),
            vmem((chunks, CHUNK), F32),
            vmem((nh, chunks, CHUNK), F32),
            pltpu.SemaphoreType.DMA((7,)),
            pltpu.SemaphoreType.DMA((4,)),
            pltpu.SemaphoreType.DMA((4,)),
        ],
        compiler_params=pltpu.CompilerParams(
            collective_id=0, has_side_effects=True, vmem_limit_bytes=24 << 20
        ),
    )(*(
        pltpu.with_memory_space_constraint(operand, hbm)
        for operand in (lengths, skip_coef, head_inputs, gate_z, input_b, output_c, log_decay.T)
    ))
    return pl.pallas_call(
        normalize,
        out_shape=jax.ShapeDtypeStruct((tokens, lanes), BF16),
        in_specs=[pl.BlockSpec(memory_space=vmem)] * 3,
        out_specs=pl.BlockSpec(memory_space=hbm),
        scratch_shapes=[vmem((tokens, lanes), BF16), pltpu.SemaphoreType.DMA((chunks,))],
        compiler_params=pltpu.CompilerParams(vmem_limit_bytes=8 << 20),
    )(gated, scales, norm_gain.reshape(1, lanes))


def solution(mesh):
    return jax.shard_map(
        functools.partial(on_device, mesh.shape["head"], mesh.shape["ctx"]),
        mesh=mesh,
        in_specs=(
            P("ctx", "head"),
            P("ctx", "head"),
            P("ctx", None),
            P("ctx", None),
            P("ctx", "head"),
            P(),
            P("head"),
            P("head"),
        ),
        out_specs=P("ctx", "head"),
        check_vma=False,
    )
```

time: 43.6 us -> 37.6 us (0.86)
  Pallas kernels: 41.2 us -> 37.4 us
  local copies, waits for them, and re-layouts: 2.26 us -> 0.01 us
    pallas_call x1, Pallas kernels: 41.2 us -> 36.3 us  [on_device(): pl.pallas_call(functools.partial(kernel, nh, nc, heads * nh // groups), o...]
    unnamed x1 -> x2, local copies, waits for them, and re-layouts: 2.26 us -> 0.01 us
    pallas_call x0 -> x1, Pallas kernels: none -> 1.14 us  [on_device(): pl.pallas_call(normalize, out_shape=jax.ShapeDtypeStruct((tokens, lanes),...]
where the time goes in v2:
time: 37.6 us; the launch traced here: 37.5 us
  Pallas kernels  37.4 us (99%)
    pallas_call x1, Pallas kernels, on_device(): pl.pallas_call(functools.partial(kernel, nh, nc, heads * nh // groups), o...  36.3 us
    pallas_call x1, Pallas kernels, on_device(): pl.pallas_call(normalize, out_shape=jax.ShapeDtypeStruct((tokens, lanes),...  1.14 us

profile of v2, /device:TPU:1, one launch (start us, length us, event | category | flops | bytes accessed | tf_op | source)
XLA Modules:
  0.0 37.5 jit_solution(4526562204671965118)
XLA Ops:
  0.0 0.0 copy-start
  0.0 36.3 %shard_map.82 = (f32[1024,512]{1,0:T(8,128)S(1)}, f32[8,128]{1,0:T(8,128)S(1)}) custom-call(s32[16]{0:T(128)} %lengths_hbm.1, f32[8]{0:T(128)} %skip_hbm.1, bf16[1024,512]{1,0:T(8,128)(2,1)} %x_hbm.1, bf16[1024,512]{1,0:T(8,128)(2,1)} %z_hbm.1, bf16[1024,1024]{1,0:T(8,128)(2,1)} %b_hbm.1, bf16[1024,1024]{1,0:T(8,128)(2,1)} %c_hbm.1, f32[8,1024]{1,0:T(8,128)} %bitcast.3), custom_call_target="tpu_custom_call" | custom-call | tf_op jit(solution)/shard_map/pallas_call | solution.py:296
  36.3 0.0 copy-done
  36.3 1.1 %shard_map.83 = bf16[1024,512]{1,0:T(8,128)(2,1)} custom-call(f32[1024,512]{1,0:T(8,128)S(1)} %get-tuple-element.7.gated, f32[8,128]{1,0:T(8,128)S(1)} %get-tuple-element.8.scales, f32[1,512]{1,0:T(1,128)S(1)} %bitcast.2), custom_call_target="tpu_custom_call" | custom-call | tf_op jit(solution)/shard_map/pallas_call | solution.py:342
Async XLA Ops:
  0.0 36.3 %copy-start = (f32[512]{0:T(512)S(1)}, f32[512]{0:T(512)}, u32[]{:S(2)}) copy-start(f32[512]{0:T(512)} %param.15) | copy-start | bytes 6148

commit v3 on v2

--- a/solution.py
+++ b/solution.py
@@ -35,7 +35,7 @@
     nh, nc, group_heads, lengths_hbm, skip_hbm, x_hbm, z_hbm, b_hbm, c_hbm, decay_hbm, gated, scales,
     lengths, skip, x, z, b, c, b_turned, decay, table, spread, spread_request, requests, leaving, local_state, state,
     partial, gate, from_device, decay_out, decay_in, slice_out, slice_in, enter_out, enter_in,
-    square_out, square_in, load_sem, send_sem, recv_sem,
+    square_out, square_in, load_sem, send_sem, recv_sem, ready,
 ):
     head_pos = lax.axis_index("head")
     ctx_pos = lax.axis_index("ctx")
@@ -60,17 +60,20 @@
 
     barrier = pltpu.get_barrier_semaphore()
 
-    def greet(axis, place, count):
-        def one(step, carry):
+    def greet(step, carry):
+        other = lax.rem(ctx_pos + step, nc)
+        pl.semaphore_signal(barrier, inc=1, device_id={"ctx": other}, device_id_type=MESH)
+        return carry
+
+    def signal_heads(semaphore, distance):
+        for offset in (distance, nh - distance):
             pl.semaphore_signal(
-                barrier, inc=1, device_id={axis: lax.rem(place + step, count)}, device_id_type=MESH
+                semaphore, inc=1, device_id={"head": lax.rem(head_pos + offset, nh)}, device_id_type=MESH
             )
-            return carry
-
-        lax.fori_loop(1, count, one, 0)
-
-    greet("ctx", ctx_pos, nc)
-    greet("head", head_pos, nh)
+
+    lax.fori_loop(1, nc, greet, 0)
+    signal_heads(barrier, 1)
+    rounds = [2**i for i in range(nh.bit_length()) if 2 * 2**i < nh]
 
     def send(axis, place, other, source, target, which):
         pltpu.make_async_remote_copy(
@@ -184,7 +187,9 @@
         for i in range(nc // 2):
             slice_out[2 * i + half] = entering[i * share_rows : (i + 1) * share_rows]
         if half == 0:
-            pl.semaphore_wait(barrier, nc - 1 + nh - 1)
+            pl.semaphore_wait(barrier, nc - 1 + 2)
+            if rounds:
+                signal_heads(ready.at[0], rounds[0])
             for which_core in range(2):
                 send_to_core(which_core, lambda other: decay_out, decay_in, 0)
         send_to_core(half, lambda other: slice_out.at[other], slice_in, 1)
@@ -220,6 +225,14 @@
 
     lax.fori_loop(0, chunks, own_part, 0)
 
+    def hear(i):
+        pl.semaphore_wait(ready.at[i], 2)
+        if i + 1 < len(rounds):
+            signal_heads(ready.at[i + 1], rounds[i + 1])
+
+    for i in range(len(rounds))[:1]:
+        hear(i)
+
     for target, which in ((decay_in, 0), (slice_in, 1)):
         arrived = arrival("ctx", ctx_pos, nc, target, which)
         arrived.wait_recv()
@@ -233,6 +246,8 @@
         entering = steps[i : i + 1] * entering + slice_in[i]
     for which_core in range(2):
         send_to_core(which_core, lambda other: enter_out.at[other], enter_in, 2)
+    for i in range(len(rounds))[1:2]:
+        hear(i)
     enter_in[ctx_pos] = enter_out[ctx_pos]
     arrived = arrival("ctx", ctx_pos, nc, enter_in, 2)
     arrived.wait_recv()
@@ -256,6 +271,8 @@
                 folded[i * CHUNK : (i + 1) * CHUNK].T, axis=0, keepdims=True
             )
 
+    for i in range(len(rounds))[2:]:
+        hear(i)
     for offset in sorted(range(1, nh), key=lambda offset: -around(offset, nh)):
         send("head", head_pos, lax.rem(head_pos + offset, nh), square_out, square_in, 3)
     square_in[head_pos] = square_out[...]
@@ -331,6 +348,7 @@
             pltpu.SemaphoreType.DMA((7,)),
             pltpu.SemaphoreType.DMA((4,)),
             pltpu.SemaphoreType.DMA((4,)),
+            pltpu.SemaphoreType.REGULAR((4,)),
         ],
         compiler_params=pltpu.CompilerParams(
             collective_id=0, has_side_effects=True, vmem_limit_bytes=24 << 20

time: 37.6 us -> 37.2 us (0.989)
  no operation moved by 1% of the time
where the time goes in v3:
time: 37.2 us; the launch traced here: 37.1 us
  Pallas kernels  37.1 us (100%)
    pallas_call x1, Pallas kernels, on_device(): pl.pallas_call(functools.partial(kernel, nh, nc, heads * nh // groups), o...  36 us
    pallas_call x1, Pallas kernels, on_device(): pl.pallas_call(normalize, out_shape=jax.ShapeDtypeStruct((tokens, lanes),...  1.14 us

profile of v3, /device:TPU:1, one launch (start us, length us, event | category | flops | bytes accessed | tf_op | source)
XLA Modules:
  0.0 37.1 jit_solution(12981924746414896867)
XLA Ops:
  0.0 0.0 copy-start
  0.0 36.0 %shard_map.82 = (f32[1024,512]{1,0:T(8,128)S(1)}, f32[8,128]{1,0:T(8,128)S(1)}) custom-call(s32[16]{0:T(128)} %lengths_hbm.1, f32[8]{0:T(128)} %skip_hbm.1, bf16[1024,512]{1,0:T(8,128)(2,1)} %x_hbm.1, bf16[1024,512]{1,0:T(8,128)(2,1)} %z_hbm.1, bf16[1024,1024]{1,0:T(8,128)(2,1)} %b_hbm.1, bf16[1024,1024]{1,0:T(8,128)(2,1)} %c_hbm.1, f32[8,1024]{1,0:T(8,128)} %bitcast.3), custom_call_target="tpu_custom_call" | custom-call | tf_op jit(solution)/shard_map/pallas_call | solution.py:313
  36.0 0.0 copy-done
  36.0 1.1 %shard_map.83 = bf16[1024,512]{1,0:T(8,128)(2,1)} custom-call(f32[1024,512]{1,0:T(8,128)S(1)} %get-tuple-element.7.gated, f32[8,128]{1,0:T(8,128)S(1)} %get-tuple-element.8.scales, f32[1,512]{1,0:T(1,128)S(1)} %bitcast.2), custom_call_target="tpu_custom_call" | custom-call | tf_op jit(solution)/shard_map/pallas_call | solution.py:360
Async XLA Ops:
  0.0 36.0 %copy-start = (f32[512]{0:T(512)S(1)}, f32[512]{0:T(512)}, u32[]{:S(2)}) copy-start(f32[512]{0:T(512)} %param.15) | copy-start | bytes 6148

commit v4 on v3

--- a/solution.py
+++ b/solution.py
@@ -93,18 +93,21 @@
         key=lambda hop: -around(hop[0], side) - around(hop[1], side),
     )
 
-    def send_to_core(which_core, source, target, which):
+    def send_to_core(which_core, source, target, which, first_too=True):
         for down, along in hops:
             chip = lax.rem(chip_row + down, side) * side + lax.rem(chip_column + along, side)
             other = 2 * chip + which_core
+            wanted = True if first_too else chip != 0
             if (down, along) == (0, 0):
-
-                @pl.when(core != which_core)
-                def _():
-                    send("ctx", ctx_pos, other, source(other), target, which)
-
+                wanted &= core != which_core
+
+            def one(other=other):
+                send("ctx", ctx_pos, other, source(other), target, which)
+
+            if wanted is True:
+                one()
             else:
-                send("ctx", ctx_pos, other, source(other), target, which)
+                pl.when(wanted)(one)
 
     def arrival(axis, place, count, target, which):
         return pltpu.make_async_remote_copy(
@@ -193,6 +196,15 @@
             for which_core in range(2):
                 send_to_core(which_core, lambda other: decay_out, decay_in, 0)
         send_to_core(half, lambda other: slice_out.at[other], slice_in, 1)
+    first_copy = pltpu.make_async_remote_copy(
+        src_ref=slice_out,
+        dst_ref=enter_in,
+        send_sem=send_sem.at[4],
+        recv_sem=recv_sem.at[4],
+        device_id={"ctx": 1 - core},
+        device_id_type=MESH,
+    )
+    pl.when(ctx_pos == 0)(first_copy.start)
     decay_in[ctx_pos] = decay_out[...]
     slice_in[ctx_pos] = slice_out[ctx_pos]
 
@@ -245,12 +257,24 @@
         enter_out[i] = entering
         entering = steps[i : i + 1] * entering + slice_in[i]
     for which_core in range(2):
-        send_to_core(which_core, lambda other: enter_out.at[other], enter_in, 2)
+        send_to_core(which_core, lambda other: enter_out.at[other], enter_in, 2, first_too=False)
     for i in range(len(rounds))[1:2]:
         hear(i)
-    enter_in[ctx_pos] = enter_out[ctx_pos]
     arrived = arrival("ctx", ctx_pos, nc, enter_in, 2)
-    arrived.wait_recv()
+
+    @pl.when(ctx_pos == 0)
+    def _():
+        enter_in[...] = jnp.zeros(enter_in.shape, F32)
+
+    @pl.when(ctx_pos == 1)
+    def _():
+        first_copy.wait_recv()
+
+    @pl.when(ctx_pos >= 2)
+    def _():
+        enter_in[ctx_pos] = enter_out[ctx_pos]
+        arrived.wait_recv()
+
     for half in range(2):
         for i in range(nc // 2):
             state[i * share_rows : (i + 1) * share_rows, half * share : (half + 1) * share] = enter_in[2 * i + half]
@@ -276,7 +300,32 @@
     for offset in sorted(range(1, nh), key=lambda offset: -around(offset, nh)):
         send("head", head_pos, lax.rem(head_pos + offset, nh), square_out, square_in, 3)
     square_in[head_pos] = square_out[...]
-    arrived.wait_send()
+    sent = pltpu.make_async_remote_copy(
+        src_ref=enter_out.at[pl.ds(0, nc - 3)],
+        dst_ref=enter_out.at[pl.ds(0, nc - 3)],
+        send_sem=send_sem.at[2],
+        recv_sem=recv_sem.at[2],
+        device_id={"ctx": 1 - core},
+        device_id_type=MESH,
+    )
+
+    @pl.when(ctx_pos == 0)
+    def _():
+        first_copy.wait_send()
+
+    sent.wait_send()
+
+    @pl.when(ctx_pos < 2)
+    def _():
+        pltpu.make_async_remote_copy(
+            src_ref=enter_out.at[0],
+            dst_ref=enter_out.at[0],
+            send_sem=send_sem.at[2],
+            recv_sem=recv_sem.at[2],
+            device_id={"ctx": 1 - core},
+            device_id_type=MESH,
+        ).wait_send()
+
     arrived = arrival("head", head_pos, nh, square_in, 3)
     arrived.wait_recv()
     squares = square_in[0]
@@ -346,8 +395,8 @@
             vmem((chunks, CHUNK), F32),
             vmem((nh, chunks, CHUNK), F32),
             pltpu.SemaphoreType.DMA((7,)),
-            pltpu.SemaphoreType.DMA((4,)),
-            pltpu.SemaphoreType.DMA((4,)),
+            pltpu.SemaphoreType.DMA((5,)),
+            pltpu.SemaphoreType.DMA((5,)),
             pltpu.SemaphoreType.REGULAR((4,)),
         ],
         compiler_params=pltpu.CompilerParams(

time: 37.2 us -> 35 us (0.941)
  the two profiles are of different devices: /device:TPU:1 before, /device:TPU:7 now
where the time goes in v4:
time: 35 us; the launch traced here: 34.6 us
  Pallas kernels  34.6 us (99%)
    pallas_call x1, Pallas kernels, on_device(): pl.pallas_call(functools.partial(kernel, nh, nc, heads * nh // groups), o...  33.4 us
    pallas_call x1, Pallas kernels, on_device(): pl.pallas_call(normalize, out_shape=jax.ShapeDtypeStruct((tokens, lanes),...  1.14 us

profile of v4, /device:TPU:7, one launch (start us, length us, event | category | flops | bytes accessed | tf_op | source)
XLA Modules:
  0.0 34.6 jit_solution(13874480925941001230)
XLA Ops:
  0.0 0.0 copy-start
  0.0 33.4 %shard_map.82 = (f32[1024,512]{1,0:T(8,128)S(1)}, f32[8,128]{1,0:T(8,128)S(1)}) custom-call(s32[16]{0:T(128)} %lengths_hbm.1, f32[8]{0:T(128)} %skip_hbm.1, bf16[1024,512]{1,0:T(8,128)(2,1)} %x_hbm.1, bf16[1024,512]{1,0:T(8,128)(2,1)} %z_hbm.1, bf16[1024,1024]{1,0:T(8,128)(2,1)} %b_hbm.1, bf16[1024,1024]{1,0:T(8,128)(2,1)} %c_hbm.1, f32[8,1024]{1,0:T(8,128)} %bitcast.3), custom_call_target="tpu_custom_call" | custom-call | tf_op jit(solution)/shard_map/pallas_call | solution.py:362
  33.5 0.0 copy-done
  33.5 1.1 %shard_map.83 = bf16[1024,512]{1,0:T(8,128)(2,1)} custom-call(f32[1024,512]{1,0:T(8,128)S(1)} %get-tuple-element.7.gated, f32[8,128]{1,0:T(8,128)S(1)} %get-tuple-element.8.scales, f32[1,512]{1,0:T(1,128)S(1)} %bitcast.2), custom_call_target="tpu_custom_call" | custom-call | tf_op jit(solution)/shard_map/pallas_call | solution.py:409
Async XLA Ops:
  0.0 33.5 %copy-start = (f32[512]{0:T(512)S(1)}, f32[512]{0:T(512)}, u32[]{:S(2)}) copy-start(f32[512]{0:T(512)} %param.15) | copy-start | bytes 6148

commit v5 on v3

--- a/solution.py
+++ b/solution.py
@@ -16,6 +16,7 @@
 TO_END, TO_KEY, TO_QUERY, FROM_CHUNK, FROM_DEVICE = range(5)
 KINDS = 5
 REQUEST_ROW = KINDS * ROWS
+DECAY, FIRST_HALF, SECOND_HALF, STEP_BEFORE, SLICE_BEFORE, STEP, SLICE, ENTER, SWAP, SQUARE = range(10)
 F32, BF16 = jnp.float32, jnp.bfloat16
 
 
@@ -34,8 +35,9 @@
 def kernel(
     nh, nc, group_heads, lengths_hbm, skip_hbm, x_hbm, z_hbm, b_hbm, c_hbm, decay_hbm, gated, scales,
     lengths, skip, x, z, b, c, b_turned, decay, table, spread, spread_request, requests, leaving, local_state, state,
-    partial, gate, from_device, decay_out, decay_in, slice_out, slice_in, enter_out, enter_in,
-    square_out, square_in, load_sem, send_sem, recv_sem, ready,
+    partial, gate, from_device, decay_out, decay_in, decays, state_out, state_in, step_out, step_in,
+    slice_out, slice_in, enter_out, enter_in, enter_other, square_out, square_in,
+    load_sem, send_sem, recv_sem, ready,
 ):
     head_pos = lax.axis_index("head")
     ctx_pos = lax.axis_index("ctx")
@@ -60,10 +62,17 @@
 
     barrier = pltpu.get_barrier_semaphore()
 
-    def greet(step, carry):
-        other = lax.rem(ctx_pos + step, nc)
+    side = math.isqrt(nc // 2)
+    core = lax.rem(ctx_pos, 2)
+    chip = ctx_pos // 2
+    chip_row, chip_column = chip // side, lax.rem(chip, side)
+    not_first_row, not_last_row = chip_row > 0, chip_row < side - 1
+
+    def device_at(down, along):
+        return (lax.rem(chip_row + down, side) * side + lax.rem(chip_column + along, side)) * 2 + core
+
+    def signal_ctx(other):
         pl.semaphore_signal(barrier, inc=1, device_id={"ctx": other}, device_id_type=MESH)
-        return carry
 
     def signal_heads(semaphore, distance):
         for offset in (distance, nh - distance):
@@ -71,50 +80,42 @@
                 semaphore, inc=1, device_id={"head": lax.rem(head_pos + offset, nh)}, device_id_type=MESH
             )
 
-    lax.fori_loop(1, nc, greet, 0)
+    signal_ctx(ctx_pos + 1 - 2 * core)
+    for along in range(1, side):
+        signal_ctx(device_at(0, along))
+    for along in range(side):
+        signal_ctx(device_at(side - 1, along))
     signal_heads(barrier, 1)
     rounds = [2**i for i in range(nh.bit_length()) if 2 * 2**i < nh]
 
-    def send(axis, place, other, source, target, which):
-        pltpu.make_async_remote_copy(
+    waits = []
+
+    def send(device, source, target, which, condition=None):
+        copy = pltpu.make_async_remote_copy(
             src_ref=source,
-            dst_ref=target.at[place],
-            send_sem=send_sem.at[which],
+            dst_ref=target,
+            send_sem=send_sem.at[len(waits)],
             recv_sem=recv_sem.at[which],
-            device_id={axis: other},
-            device_id_type=MESH,
-        ).start()
-
-    side = math.isqrt(nc // 2)
-    core = lax.rem(ctx_pos, 2)
-    chip_row, chip_column = ctx_pos // (2 * side), lax.rem(ctx_pos // 2, side)
-    hops = sorted(
-        ((i, j) for i in range(side) for j in range(side)),
-        key=lambda hop: -around(hop[0], side) - around(hop[1], side),
-    )
-
-    def send_to_core(which_core, source, target, which):
-        for down, along in hops:
-            chip = lax.rem(chip_row + down, side) * side + lax.rem(chip_column + along, side)
-            other = 2 * chip + which_core
-            if (down, along) == (0, 0):
-
-                @pl.when(core != which_core)
-                def _():
-                    send("ctx", ctx_pos, other, source(other), target, which)
-
-            else:
-                send("ctx", ctx_pos, other, source(other), target, which)
-
-    def arrival(axis, place, count, target, which):
-        return pltpu.make_async_remote_copy(
-            src_ref=target.at[pl.ds(0, count - 1)],
-            dst_ref=target.at[pl.ds(0, count - 1)],
-            send_sem=send_sem.at[which],
-            recv_sem=recv_sem.at[which],
-            device_id={axis: lax.rem(place + 1, count)},
+            device_id=device,
             device_id_type=MESH,
         )
+        waits.append((copy, condition))
+        if condition is None:
+            copy.start()
+        else:
+            pl.when(condition)(copy.start)
+
+    def await_bytes(buffer, which):
+        pltpu.make_async_remote_copy(
+            src_ref=buffer,
+            dst_ref=buffer,
+            send_sem=send_sem.at[0],
+            recv_sem=recv_sem.at[which],
+            device_id={"ctx": ctx_pos + 1 - 2 * core},
+            device_id_type=MESH,
+        ).wait_recv()
+
+    twin = {"ctx": ctx_pos + 1 - 2 * core}
 
     loads[6].wait()
     starts = []
@@ -184,17 +185,50 @@
             local_state[k, :, part] = entering.astype(BF16)
             scaled = (x[rows, part].astype(F32) * matmul(table[k], spread[TO_END, :, part])).astype(BF16)
             entering = leaving[16 * k + 15 : 16 * k + 16, part] * entering + matmul(b_turned[k], scaled)
-        for i in range(nc // 2):
-            slice_out[2 * i + half] = entering[i * share_rows : (i + 1) * share_rows]
+        state_out[half] = entering
         if half == 0:
-            pl.semaphore_wait(barrier, nc - 1 + 2)
+            pl.semaphore_wait(barrier, 2 * side + 2)
             if rounds:
                 signal_heads(ready.at[0], rounds[0])
-            for which_core in range(2):
-                send_to_core(which_core, lambda other: decay_out, decay_in, 0)
-        send_to_core(half, lambda other: slice_out.at[other], slice_in, 1)
-    decay_in[ctx_pos] = decay_out[...]
-    slice_in[ctx_pos] = slice_out[ctx_pos]
+            send(twin, decay_out, decay_in, DECAY)
+        send(twin, state_out.at[half], state_in.at[half], FIRST_HALF + half, None if half == 0 else core == 0)
+
+    await_bytes(decay_in, DECAY)
+    both = jnp.concatenate([decay_out[...], decay_in[...]] * (ROWS // 2), axis=0).astype(BF16)
+    decays[...] = matmul(both, spread[FROM_DEVICE])
+    await_bytes(state_in.at[0], FIRST_HALF)
+
+    @pl.when(core == 1)
+    def _():
+        await_bytes(state_in.at[1], SECOND_HALF)
+
+    mine = pl.ds(pl.multiple_of(core * share, share), share)
+    others = pl.ds(pl.multiple_of((1 - core) * share, share), share)
+    first_core = core == 0
+    own_state, own_decay = state_out[core], decays[0:1, mine]
+    got_state, got_decay = state_in[core], decays[1:2, mine]
+    joined = jnp.where(first_core, own_state, got_state) * jnp.where(first_core, got_decay, own_decay)
+    joined = joined + jnp.where(first_core, got_state, own_state)
+    step_out[...] = own_decay * got_decay
+    for i in range(side):
+        slice_out[i] = joined[i * share_rows : (i + 1) * share_rows]
+    for along in range(side):
+        other = device_at(1, along)
+        column = lax.rem(chip_column + along, side)
+        send({"ctx": other}, step_out, step_in.at[chip_column], STEP_BEFORE, not_last_row)
+        send({"ctx": other}, slice_out.at[column], slice_in.at[chip_column], SLICE_BEFORE, not_last_row)
+    for along in range(1, side):
+        other = device_at(0, along)
+        column = lax.rem(chip_column + along, side)
+        send({"ctx": other}, step_out, step_in.at[side + chip_column], STEP)
+        send({"ctx": other}, slice_out.at[column], slice_in.at[side + chip_column], SLICE)
+    step_in[side + chip_column] = step_out[...]
+    slice_in[side + chip_column] = slice_out[chip_column]
+
+    @pl.when(chip_row == 0)
+    def _():
+        step_in[0:side] = jnp.zeros((side, 1, share), F32)
+        slice_in[0:side] = jnp.zeros((side, share_rows, share), F32)
 
     def at(k):
         return pl.ds(pl.multiple_of(k * CHUNK, CHUNK), CHUNK)
@@ -233,27 +267,49 @@
     for i in range(len(rounds))[:1]:
         hear(i)
 
-    for target, which in ((decay_in, 0), (slice_in, 1)):
-        arrived = arrival("ctx", ctx_pos, nc, target, which)
-        arrived.wait_recv()
-        arrived.wait_send()
-    rows_in = jnp.concatenate([decay_in[i] for i in range(nc)], axis=0).astype(BF16)
-    part = pl.ds(pl.multiple_of(core * share, share), share)
-    steps = matmul(rows_in, spread[FROM_DEVICE, :, part])
-    entering = jnp.zeros((share_rows, share), F32)
-    for i in range(nc):
-        enter_out[i] = entering
-        entering = steps[i : i + 1] * entering + slice_in[i]
-    for which_core in range(2):
-        send_to_core(which_core, lambda other: enter_out.at[other], enter_in, 2)
+    @pl.when(not_first_row)
+    def _():
+        await_bytes(step_in.at[0:side], STEP_BEFORE)
+        await_bytes(slice_in.at[0:side], SLICE_BEFORE)
+
+    await_bytes(step_in.at[0 : side - 1], STEP)
+    await_bytes(slice_in.at[0 : side - 1], SLICE)
+    entering = slice_in[0]
+    for i in range(1, 2 * side):
+        if i >= side:
+            enter_out[i - side] = entering
+        entering = step_in[i] * entering + slice_in[i] if i < 2 * side - 1 else entering
+    for along in range(side - 1, 0, -1):
+        column = lax.rem(chip_column + along, side)
+        send(
+            {"ctx": device_at(0, along)}, enter_out.at[column], enter_in.at[chip_column], ENTER,
+            not_first_row | (column > 0),
+        )
     for i in range(len(rounds))[1:2]:
         hear(i)
-    enter_in[ctx_pos] = enter_out[ctx_pos]
-    arrived = arrival("ctx", ctx_pos, nc, enter_in, 2)
-    arrived.wait_recv()
-    for half in range(2):
-        for i in range(nc // 2):
-            state[i * share_rows : (i + 1) * share_rows, half * share : (half + 1) * share] = enter_in[2 * i + half]
+
+    @pl.when(chip > 0)
+    def _():
+        enter_in[chip_column] = enter_out[chip_column]
+        await_bytes(enter_in.at[0 : side - 1], ENTER)
+
+    send(twin, enter_in, enter_other, SWAP, chip > 0)
+
+    @pl.when(chip > 0)
+    def _():
+        state[:, mine] = enter_in[...].reshape(state_size, share)
+        await_bytes(enter_other, SWAP)
+        state[:, others] = enter_other[...].reshape(state_size, share)
+
+    @pl.when(chip == 0)
+    def _():
+        state[...] = jnp.zeros(state.shape, F32)
+
+    @pl.when(core == 1)
+    def _():
+        before_core = jnp.concatenate([state_in[0], state_in[1]], axis=1)
+        state[...] = decays[1:2, :] * state[...] + before_core
+
     entered = state[...].astype(BF16)
 
     step_rows = 2 * CHUNK
@@ -274,16 +330,18 @@
     for i in range(len(rounds))[2:]:
         hear(i)
     for offset in sorted(range(1, nh), key=lambda offset: -around(offset, nh)):
-        send("head", head_pos, lax.rem(head_pos + offset, nh), square_out, square_in, 3)
+        send({"head": lax.rem(head_pos + offset, nh)}, square_out, square_in.at[head_pos], SQUARE)
     square_in[head_pos] = square_out[...]
-    arrived.wait_send()
-    arrived = arrival("head", head_pos, nh, square_in, 3)
-    arrived.wait_recv()
+    await_bytes(square_in.at[0 : nh - 1], SQUARE)
     squares = square_in[0]
     for i in range(1, nh):
         squares = squares + square_in[i]
     scales[...] = lax.rsqrt(squares / (nh * lanes) + EPS)
-    arrived.wait_send()
+    for copy, condition in waits:
+        if condition is None:
+            copy.wait_send()
+        else:
+            pl.when(condition)(copy.wait_send)
 
 
 def normalize(gated, scales, gain, out_hbm, out, sem):
@@ -308,7 +366,8 @@
     groups = input_b.shape[1] // state_size
     chunks = tokens // CHUNK
     share = lanes // 2
-    share_rows = 2 * state_size // nc
+    side = math.isqrt(nc // 2)
+    share_rows = state_size // side
     vmem, smem, hbm = pltpu.VMEM, pltpu.SMEM, pltpu.HBM
     gated, scales = pl.pallas_call(
         functools.partial(kernel, nh, nc, heads * nh // groups),
@@ -338,16 +397,22 @@
             vmem((tokens, lanes), F32),
             vmem((tokens, lanes), F32),
             vmem((1, CHUNK), F32),
-            vmem((nc, 1, CHUNK), F32),
-            vmem((nc, share_rows, share), F32),
-            vmem((nc, share_rows, share), F32),
-            vmem((nc, share_rows, share), F32),
-            vmem((nc, share_rows, share), F32),
+            vmem((1, CHUNK), F32),
+            vmem((heads, lanes), F32),
+            vmem((2, state_size, share), F32),
+            vmem((2, state_size, share), F32),
+            vmem((1, share), F32),
+            vmem((2 * side, 1, share), F32),
+            vmem((side, share_rows, share), F32),
+            vmem((2 * side, share_rows, share), F32),
+            vmem((side, share_rows, share), F32),
+            vmem((side, share_rows, share), F32),
+            vmem((side, share_rows, share), F32),
             vmem((chunks, CHUNK), F32),
             vmem((nh, chunks, CHUNK), F32),
             pltpu.SemaphoreType.DMA((7,)),
-            pltpu.SemaphoreType.DMA((4,)),
-            pltpu.SemaphoreType.DMA((4,)),
+            pltpu.SemaphoreType.DMA((6 * side + nh + 4,)),
+            pltpu.SemaphoreType.DMA((10,)),
             pltpu.SemaphoreType.REGULAR((4,)),
         ],
         compiler_params=pltpu.CompilerParams(

time: 37.2 us -> 35.5 us (0.954)
  the two profiles are of different devices: /device:TPU:1 before, /device:TPU:4 now
where the time goes in v5:
time: 35.5 us; the launch traced here: 35.4 us
  Pallas kernels  35.4 us (100%)
    pallas_call x1, Pallas kernels, on_device(): pl.pallas_call(functools.partial(kernel, nh, nc, heads * nh // groups), o...  34.2 us
    pallas_call x1, Pallas kernels, on_device(): pl.pallas_call(normalize, out_shape=jax.ShapeDtypeStruct((tokens, lanes),...  1.14 us

profile of v5, /device:TPU:4, one launch (start us, length us, event | category | flops | bytes accessed | tf_op | source)
XLA Modules:
  0.0 35.4 jit_solution(4387800623487121076)
XLA Ops:
  0.0 0.0 copy-start
  0.0 34.2 %shard_map.82 = (f32[1024,512]{1,0:T(8,128)S(1)}, f32[8,128]{1,0:T(8,128)S(1)}) custom-call(s32[16]{0:T(128)} %lengths_hbm.1, f32[8]{0:T(128)} %skip_hbm.1, bf16[1024,512]{1,0:T(8,128)(2,1)} %x_hbm.1, bf16[1024,512]{1,0:T(8,128)(2,1)} %z_hbm.1, bf16[1024,1024]{1,0:T(8,128)(2,1)} %b_hbm.1, bf16[1024,1024]{1,0:T(8,128)(2,1)} %c_hbm.1, f32[8,1024]{1,0:T(8,128)} %bitcast.3), custom_call_target="tpu_custom_call" | custom-call | tf_op jit(solution)/shard_map/pallas_call | solution.py:372
  34.2 0.0 copy-done
  34.2 1.1 %shard_map.83 = bf16[1024,512]{1,0:T(8,128)(2,1)} custom-call(f32[1024,512]{1,0:T(8,128)S(1)} %get-tuple-element.7.gated, f32[8,128]{1,0:T(8,128)S(1)} %get-tuple-element.8.scales, f32[1,512]{1,0:T(1,128)S(1)} %bitcast.2), custom_call_target="tpu_custom_call" | custom-call | tf_op jit(solution)/shard_map/pallas_call | solution.py:425
Async XLA Ops:
  0.0 34.2 %copy-start = (f32[512]{0:T(512)S(1)}, f32[512]{0:T(512)}, u32[]{:S(2)}) copy-start(f32[512]{0:T(512)} %param.15) | copy-start | bytes 6148

commit v6 on v5

--- a/solution.py
+++ b/solution.py
@@ -177,8 +177,9 @@
     for k in range(chunks):
         b_turned[k] = b[k * CHUNK : (k + 1) * CHUNK, :].T
     loads[2].wait()
-    for half in range(2):
-        part = slice(half * share, (half + 1) * share)
+    mine = pl.ds(pl.multiple_of(core * share, share), share)
+    others = pl.ds(pl.multiple_of((1 - core) * share, share), share)
+    for half, part, which in ((1 - core, others, FIRST_HALF), (core, mine, SECOND_HALF)):
         entering = jnp.zeros((state_size, share), F32)
         for k in range(chunks):
             rows = slice(k * CHUNK, (k + 1) * CHUNK)
@@ -186,24 +187,17 @@
             scaled = (x[rows, part].astype(F32) * matmul(table[k], spread[TO_END, :, part])).astype(BF16)
             entering = leaving[16 * k + 15 : 16 * k + 16, part] * entering + matmul(b_turned[k], scaled)
         state_out[half] = entering
-        if half == 0:
+        if which == FIRST_HALF:
             pl.semaphore_wait(barrier, 2 * side + 2)
             if rounds:
                 signal_heads(ready.at[0], rounds[0])
             send(twin, decay_out, decay_in, DECAY)
-        send(twin, state_out.at[half], state_in.at[half], FIRST_HALF + half, None if half == 0 else core == 0)
+        send(twin, state_out.at[half], state_in.at[half], which, None if which == FIRST_HALF else core == 0)
 
     await_bytes(decay_in, DECAY)
     both = jnp.concatenate([decay_out[...], decay_in[...]] * (ROWS // 2), axis=0).astype(BF16)
     decays[...] = matmul(both, spread[FROM_DEVICE])
     await_bytes(state_in.at[0], FIRST_HALF)
-
-    @pl.when(core == 1)
-    def _():
-        await_bytes(state_in.at[1], SECOND_HALF)
-
-    mine = pl.ds(pl.multiple_of(core * share, share), share)
-    others = pl.ds(pl.multiple_of((1 - core) * share, share), share)
     first_core = core == 0
     own_state, own_decay = state_out[core], decays[0:1, mine]
     got_state, got_decay = state_in[core], decays[1:2, mine]
@@ -212,12 +206,12 @@
     step_out[...] = own_decay * got_decay
     for i in range(side):
         slice_out[i] = joined[i * share_rows : (i + 1) * share_rows]
-    for along in range(side):
+    for along in sorted(range(side), key=lambda along: -around(along, side)):
         other = device_at(1, along)
         column = lax.rem(chip_column + along, side)
         send({"ctx": other}, step_out, step_in.at[chip_column], STEP_BEFORE, not_last_row)
         send({"ctx": other}, slice_out.at[column], slice_in.at[chip_column], SLICE_BEFORE, not_last_row)
-    for along in range(1, side):
+    for along in sorted(range(1, side), key=lambda along: -around(along, side)):
         other = device_at(0, along)
         column = lax.rem(chip_column + along, side)
         send({"ctx": other}, step_out, step_in.at[side + chip_column], STEP)
@@ -229,9 +223,6 @@
     def _():
         step_in[0:side] = jnp.zeros((side, 1, share), F32)
         slice_in[0:side] = jnp.zeros((side, share_rows, share), F32)
-
-    def at(k):
-        return pl.ds(pl.multiple_of(k * CHUNK, CHUNK), CHUNK)
 
     loads[3].wait()
     loads[4].wait()
@@ -242,10 +233,10 @@
         skip_row = jnp.where(lane_head == h, skip[h], skip_row)
     causal = iota((CHUNK, CHUNK), 0) >= iota((CHUNK, CHUNK), 1)
 
-    def own_part(k, carry):
-        rows = at(k)
+    def own_part(k):
+        rows = slice(k * CHUNK, (k + 1) * CHUNK)
         maps = c[rows, :]
-        same = matmul(table[k], spread_request[...]) == requests[pl.ds(k, 1), :]
+        same = matmul(table[k], spread_request[...]) == requests[k : k + 1, :]
         scores = jnp.where(causal & same, matmul(maps, b_turned[k]), 0.0).astype(BF16)
         wide = x[rows, :].astype(F32)
         keys = (wide * matmul(table[k], spread[TO_KEY])).astype(BF16)
@@ -255,9 +246,9 @@
         from_device[rows, :] = matmul(table[k], spread[FROM_DEVICE])
         branch = z[rows, :].astype(F32)
         gate[rows, :] = branch / (1.0 + jnp.exp(-branch))
-        return carry
-
-    lax.fori_loop(0, chunks, own_part, 0)
+
+    for k in range(chunks):
+        own_part(k)
 
     def hear(i):
         pl.semaphore_wait(ready.at[i], 2)
@@ -279,7 +270,7 @@
         if i >= side:
             enter_out[i - side] = entering
         entering = step_in[i] * entering + slice_in[i] if i < 2 * side - 1 else entering
-    for along in range(side - 1, 0, -1):
+    for along in sorted(range(1, side), key=lambda along: -around(along, side)):
         column = lax.rem(chip_column + along, side)
         send(
             {"ctx": device_at(0, along)}, enter_out.at[column], enter_in.at[chip_column], ENTER,
@@ -307,6 +298,7 @@
 
     @pl.when(core == 1)
     def _():
+        await_bytes(state_in.at[0], SECOND_HALF)
         before_core = jnp.concatenate([state_in[0], state_in[1]], axis=1)
         state[...] = decays[1:2, :] * state[...] + before_core
 

time: 35.5 us -> 34.7 us (0.977)
  the two profiles are of different devices: /device:TPU:4 before, /device:TPU:7 now
where the time goes in v6:
time: 34.7 us; the launch traced here: 34.1 us
  Pallas kernels  34.1 us (98%)
    pallas_call x1, Pallas kernels, on_device(): pl.pallas_call(functools.partial(kernel, nh, nc, heads * nh // groups), o...  32.9 us
    pallas_call x1, Pallas kernels, on_device(): pl.pallas_call(normalize, out_shape=jax.ShapeDtypeStruct((tokens, lanes),...  1.14 us

profile of v6, /device:TPU:7, one launch (start us, length us, event | category | flops | bytes accessed | tf_op | source)
XLA Modules:
  0.0 34.1 jit_solution(4870412710376467981)
XLA Ops:
  0.0 0.0 copy-start
  0.0 32.9 %shard_map.82 = (f32[1024,512]{1,0:T(8,128)S(1)}, f32[8,128]{1,0:T(8,128)S(1)}) custom-call(s32[16]{0:T(128)} %lengths_hbm.1, f32[8]{0:T(128)} %skip_hbm.1, bf16[1024,512]{1,0:T(8,128)(2,1)} %x_hbm.1, bf16[1024,512]{1,0:T(8,128)(2,1)} %z_hbm.1, bf16[1024,1024]{1,0:T(8,128)(2,1)} %b_hbm.1, bf16[1024,1024]{1,0:T(8,128)(2,1)} %c_hbm.1, f32[8,1024]{1,0:T(8,128)} %bitcast.3), custom_call_target="tpu_custom_call" | custom-call | tf_op jit(solution)/shard_map/pallas_call | solution.py:364
  32.9 0.0 copy-done
  32.9 1.1 %shard_map.83 = bf16[1024,512]{1,0:T(8,128)(2,1)} custom-call(f32[1024,512]{1,0:T(8,128)S(1)} %get-tuple-element.7.gated, f32[8,128]{1,0:T(8,128)S(1)} %get-tuple-element.8.scales, f32[1,512]{1,0:T(1,128)S(1)} %bitcast.2), custom_call_target="tpu_custom_call" | custom-call | tf_op jit(solution)/shard_map/pallas_call | solution.py:417
Async XLA Ops:
  0.0 32.9 %copy-start = (f32[512]{0:T(512)S(1)}, f32[512]{0:T(512)}, u32[]{:S(2)}) copy-start(f32[512]{0:T(512)} %param.15) | copy-start | bytes 6148

commit v7 on v6

--- a/solution.py
+++ b/solution.py
@@ -16,7 +16,7 @@
 TO_END, TO_KEY, TO_QUERY, FROM_CHUNK, FROM_DEVICE = range(5)
 KINDS = 5
 REQUEST_ROW = KINDS * ROWS
-DECAY, FIRST_HALF, SECOND_HALF, STEP_BEFORE, SLICE_BEFORE, STEP, SLICE, ENTER, SWAP, SQUARE = range(10)
+DECAY, FIRST_HALF, SECOND_HALF, BEFORE, STEP, SLICE, ENTER, SWAP, SQUARE = range(9)
 F32, BF16 = jnp.float32, jnp.bfloat16
 
 
@@ -36,7 +36,7 @@
     nh, nc, group_heads, lengths_hbm, skip_hbm, x_hbm, z_hbm, b_hbm, c_hbm, decay_hbm, gated, scales,
     lengths, skip, x, z, b, c, b_turned, decay, table, spread, spread_request, requests, leaving, local_state, state,
     partial, gate, from_device, decay_out, decay_in, decays, state_out, state_in, step_out, step_in,
-    slice_out, slice_in, enter_out, enter_in, enter_other, square_out, square_in,
+    slice_out, slice_in, before_out, before_in, enter_out, enter_in, enter_other, square_out, square_in,
     load_sem, send_sem, recv_sem, ready,
 ):
     head_pos = lax.axis_index("head")
@@ -83,8 +83,7 @@
     signal_ctx(ctx_pos + 1 - 2 * core)
     for along in range(1, side):
         signal_ctx(device_at(0, along))
-    for along in range(side):
-        signal_ctx(device_at(side - 1, along))
+    signal_ctx(device_at(side - 1, 0))
     signal_heads(barrier, 1)
     rounds = [2**i for i in range(nh.bit_length()) if 2 * 2**i < nh]
 
@@ -188,7 +187,7 @@
             entering = leaving[16 * k + 15 : 16 * k + 16, part] * entering + matmul(b_turned[k], scaled)
         state_out[half] = entering
         if which == FIRST_HALF:
-            pl.semaphore_wait(barrier, 2 * side + 2)
+            pl.semaphore_wait(barrier, side + 3)
             if rounds:
                 signal_heads(ready.at[0], rounds[0])
             send(twin, decay_out, decay_in, DECAY)
@@ -206,23 +205,13 @@
     step_out[...] = own_decay * got_decay
     for i in range(side):
         slice_out[i] = joined[i * share_rows : (i + 1) * share_rows]
-    for along in sorted(range(side), key=lambda along: -around(along, side)):
-        other = device_at(1, along)
-        column = lax.rem(chip_column + along, side)
-        send({"ctx": other}, step_out, step_in.at[chip_column], STEP_BEFORE, not_last_row)
-        send({"ctx": other}, slice_out.at[column], slice_in.at[chip_column], SLICE_BEFORE, not_last_row)
     for along in sorted(range(1, side), key=lambda along: -around(along, side)):
         other = device_at(0, along)
         column = lax.rem(chip_column + along, side)
-        send({"ctx": other}, step_out, step_in.at[side + chip_column], STEP)
-        send({"ctx": other}, slice_out.at[column], slice_in.at[side + chip_column], SLICE)
-    step_in[side + chip_column] = step_out[...]
-    slice_in[side + chip_column] = slice_out[chip_column]
-
-    @pl.when(chip_row == 0)
-    def _():
-        step_in[0:side] = jnp.zeros((side, 1, share), F32)
-        slice_in[0:side] = jnp.zeros((side, share_rows, share), F32)
+        send({"ctx": other}, step_out, step_in.at[chip_column], STEP)
+        send({"ctx": other}, slice_out.at[column], slice_in.at[chip_column], SLICE)
+    step_in[chip_column] = step_out[...]
+    slice_in[chip_column] = slice_out[chip_column]
 
     loads[3].wait()
     loads[4].wait()
@@ -258,18 +247,27 @@
     for i in range(len(rounds))[:1]:
         hear(i)
 
-    @pl.when(not_first_row)
-    def _():
-        await_bytes(step_in.at[0:side], STEP_BEFORE)
-        await_bytes(slice_in.at[0:side], SLICE_BEFORE)
-
     await_bytes(step_in.at[0 : side - 1], STEP)
     await_bytes(slice_in.at[0 : side - 1], SLICE)
-    entering = slice_in[0]
-    for i in range(1, 2 * side):
-        if i >= side:
-            enter_out[i - side] = entering
-        entering = step_in[i] * entering + slice_in[i] if i < 2 * side - 1 else entering
+    leaving_row = slice_in[0]
+    for i in range(1, side):
+        leaving_row = step_in[i] * leaving_row + slice_in[i]
+    before_out[...] = leaving_row
+    send({"ctx": device_at(1, 0)}, before_out, before_in, BEFORE, not_last_row)
+
+    @pl.when(not_first_row)
+    def _():
+        await_bytes(before_in, BEFORE)
+
+    @pl.when(chip_row == 0)
+    def _():
+        before_in[...] = jnp.zeros(before_in.shape, F32)
+
+    entering = before_in[...]
+    for i in range(side):
+        enter_out[i] = entering
+        if i < side - 1:
+            entering = step_in[i] * entering + slice_in[i]
     for along in sorted(range(1, side), key=lambda along: -around(along, side)):
         column = lax.rem(chip_column + along, side)
         send(
@@ -394,9 +392,11 @@
             vmem((2, state_size, share), F32),
             vmem((2, state_size, share), F32),
             vmem((1, share), F32),
-            vmem((2 * side, 1, share), F32),
+            vmem((side, 1, share), F32),
             vmem((side, share_rows, share), F32),
-            vmem((2 * side, share_rows, share), F32),
+            vmem((side, share_rows, share), F32),
+            vmem((share_rows, share), F32),
+            vmem((share_rows, share), F32),
             vmem((side, share_rows, share), F32),
             vmem((side, share_rows, share), F32),
             vmem((side, share_rows, share), F32),

time: 34.7 us -> 35 us (level); the launches traced: 34.1 us -> 34.8 us
  Pallas kernels: 34.1 us -> 34.8 us
    pallas_call x1, Pallas kernels: 32.9 us -> 33.7 us  [on_device(): pl.pallas_call(functools.partial(kernel, nh, nc, heads * nh // groups), o...]
where the time goes in v7:
time: 35 us; the launch traced here: 34.8 us
  Pallas kernels  34.8 us (99%)
    pallas_call x1, Pallas kernels, on_device(): pl.pallas_call(functools.partial(kernel, nh, nc, heads * nh // groups), o...  33.7 us
    pallas_call x1, Pallas kernels, on_device(): pl.pallas_call(normalize, out_shape=jax.ShapeDtypeStruct((tokens, lanes),...  1.14 us

profile of v7, /device:TPU:7, one launch (start us, length us, event | category | flops | bytes accessed | tf_op | source)
XLA Modules:
  0.0 34.8 jit_solution(14439463044667239168)
XLA Ops:
  0.0 0.0 copy-start
  0.0 33.7 %shard_map.82 = (f32[1024,512]{1,0:T(8,128)S(1)}, f32[8,128]{1,0:T(8,128)S(1)}) custom-call(s32[16]{0:T(128)} %lengths_hbm.1, f32[8]{0:T(128)} %skip_hbm.1, bf16[1024,512]{1,0:T(8,128)(2,1)} %x_hbm.1, bf16[1024,512]{1,0:T(8,128)(2,1)} %z_hbm.1, bf16[1024,1024]{1,0:T(8,128)(2,1)} %b_hbm.1, bf16[1024,1024]{1,0:T(8,128)(2,1)} %c_hbm.1, f32[8,1024]{1,0:T(8,128)} %bitcast.3), custom_call_target="tpu_custom_call" | custom-call | tf_op jit(solution)/shard_map/pallas_call | solution.py:362
  33.7 0.0 copy-done
  33.7 1.1 %shard_map.83 = bf16[1024,512]{1,0:T(8,128)(2,1)} custom-call(f32[1024,512]{1,0:T(8,128)S(1)} %get-tuple-element.7.gated, f32[8,128]{1,0:T(8,128)S(1)} %get-tuple-element.8.scales, f32[1,512]{1,0:T(1,128)S(1)} %bitcast.2), custom_call_target="tpu_custom_call" | custom-call | tf_op jit(solution)/shard_map/pallas_call | solution.py:417
Async XLA Ops:
  0.0 33.7 %copy-start = (f32[512]{0:T(512)S(1)}, f32[512]{0:T(512)}, u32[]{:S(2)}) copy-start(f32[512]{0:T(512)} %param.15) | copy-start | bytes 6148

commit v8 on v7

--- a/solution.py
+++ b/solution.py
@@ -15,6 +15,7 @@
 EPS = 1e-05
 TO_END, TO_KEY, TO_QUERY, FROM_CHUNK, FROM_DEVICE = range(5)
 KINDS = 5
+LATER = 3
 REQUEST_ROW = KINDS * ROWS
 DECAY, FIRST_HALF, SECOND_HALF, BEFORE, STEP, SLICE, ENTER, SWAP, SQUARE = range(9)
 F32, BF16 = jnp.float32, jnp.bfloat16
@@ -236,16 +237,13 @@
         branch = z[rows, :].astype(F32)
         gate[rows, :] = branch / (1.0 + jnp.exp(-branch))
 
-    for k in range(chunks):
+    for k in range(chunks - LATER):
         own_part(k)
 
     def hear(i):
         pl.semaphore_wait(ready.at[i], 2)
         if i + 1 < len(rounds):
             signal_heads(ready.at[i + 1], rounds[i + 1])
-
-    for i in range(len(rounds))[:1]:
-        hear(i)
 
     await_bytes(step_in.at[0 : side - 1], STEP)
     await_bytes(slice_in.at[0 : side - 1], SLICE)
@@ -254,6 +252,10 @@
         leaving_row = step_in[i] * leaving_row + slice_in[i]
     before_out[...] = leaving_row
     send({"ctx": device_at(1, 0)}, before_out, before_in, BEFORE, not_last_row)
+    for k in range(chunks - LATER, chunks):
+        own_part(k)
+    for i in range(len(rounds))[:1]:
+        hear(i)
 
     @pl.when(not_first_row)
     def _():

time: 35 us -> 35.1 us (level)
  no operation moved by 1% of the time
where the time goes in v8:
time: 35.1 us; the launch traced here: 35 us
  Pallas kernels  34.9 us (99%)
    pallas_call x1, Pallas kernels, on_device(): pl.pallas_call(functools.partial(kernel, nh, nc, heads * nh // groups), o...  33.8 us
    pallas_call x1, Pallas kernels, on_device(): pl.pallas_call(normalize, out_shape=jax.ShapeDtypeStruct((tokens, lanes),...  1.14 us

profile of v8, /device:TPU:7, one launch (start us, length us, event | category | flops | bytes accessed | tf_op | source)
XLA Modules:
  0.0 35.0 jit_solution(7745532921938275644)
XLA Ops:
  0.0 0.0 copy-start
  0.0 33.8 %shard_map.82 = (f32[1024,512]{1,0:T(8,128)S(1)}, f32[8,128]{1,0:T(8,128)S(1)}) custom-call(s32[16]{0:T(128)} %lengths_hbm.1, f32[8]{0:T(128)} %skip_hbm.1, bf16[1024,512]{1,0:T(8,128)(2,1)} %x_hbm.1, bf16[1024,512]{1,0:T(8,128)(2,1)} %z_hbm.1, bf16[1024,1024]{1,0:T(8,128)(2,1)} %b_hbm.1, bf16[1024,1024]{1,0:T(8,128)(2,1)} %c_hbm.1, f32[8,1024]{1,0:T(8,128)} %bitcast.3), custom_call_target="tpu_custom_call" | custom-call | tf_op jit(solution)/shard_map/pallas_call | solution.py:364
  33.8 0.0 copy-done
  33.8 1.1 %shard_map.83 = bf16[1024,512]{1,0:T(8,128)(2,1)} custom-call(f32[1024,512]{1,0:T(8,128)S(1)} %get-tuple-element.7.gated, f32[8,128]{1,0:T(8,128)S(1)} %get-tuple-element.8.scales, f32[1,512]{1,0:T(1,128)S(1)} %bitcast.2), custom_call_target="tpu_custom_call" | custom-call | tf_op jit(solution)/shard_map/pallas_call | solution.py:419
Async XLA Ops:
  0.0 33.8 %copy-start = (f32[512]{0:T(512)S(1)}, f32[512]{0:T(512)}, u32[]{:S(2)}) copy-start(f32[512]{0:T(512)} %param.15) | copy-start | bytes 6148

commit v9 on v7

--- a/solution.py
+++ b/solution.py
@@ -16,7 +16,7 @@
 TO_END, TO_KEY, TO_QUERY, FROM_CHUNK, FROM_DEVICE = range(5)
 KINDS = 5
 REQUEST_ROW = KINDS * ROWS
-DECAY, FIRST_HALF, SECOND_HALF, BEFORE, STEP, SLICE, ENTER, SWAP, SQUARE = range(9)
+DECAY, FIRST_HALF, SECOND_HALF, BEFORE, STEP, SLICE, ENTER, SQUARE = range(8)
 F32, BF16 = jnp.float32, jnp.bfloat16
 
 
@@ -36,7 +36,7 @@
     nh, nc, group_heads, lengths_hbm, skip_hbm, x_hbm, z_hbm, b_hbm, c_hbm, decay_hbm, gated, scales,
     lengths, skip, x, z, b, c, b_turned, decay, table, spread, spread_request, requests, leaving, local_state, state,
     partial, gate, from_device, decay_out, decay_in, decays, state_out, state_in, step_out, step_in,
-    slice_out, slice_in, before_out, before_in, enter_out, enter_in, enter_other, square_out, square_in,
+    slice_out, slice_in, before_out, before_in, enter_out, enter_in, square_out, square_in,
     load_sem, send_sem, recv_sem, ready,
 ):
     head_pos = lax.axis_index("head")
@@ -83,6 +83,7 @@
     signal_ctx(ctx_pos + 1 - 2 * core)
     for along in range(1, side):
         signal_ctx(device_at(0, along))
+        signal_ctx(device_at(0, along) + 1 - 2 * core)
     signal_ctx(device_at(side - 1, 0))
     signal_heads(barrier, 1)
     rounds = [2**i for i in range(nh.bit_length()) if 2 * 2**i < nh]
@@ -187,7 +188,7 @@
             entering = leaving[16 * k + 15 : 16 * k + 16, part] * entering + matmul(b_turned[k], scaled)
         state_out[half] = entering
         if which == FIRST_HALF:
-            pl.semaphore_wait(barrier, side + 3)
+            pl.semaphore_wait(barrier, 2 * side + 2)
             if rounds:
                 signal_heads(ready.at[0], rounds[0])
             send(twin, decay_out, decay_in, DECAY)
@@ -268,27 +269,23 @@
         enter_out[i] = entering
         if i < side - 1:
             entering = step_in[i] * entering + slice_in[i]
-    for along in sorted(range(1, side), key=lambda along: -around(along, side)):
+    for along in sorted(range(side), key=lambda along: -around(along, side)):
         column = lax.rem(chip_column + along, side)
-        send(
-            {"ctx": device_at(0, along)}, enter_out.at[column], enter_in.at[chip_column], ENTER,
-            not_first_row | (column > 0),
-        )
+        for turn in (0, 1) if along else (1,):
+            send(
+                {"ctx": device_at(0, along) + turn * (1 - 2 * core)}, enter_out.at[column],
+                enter_in.at[core * side + chip_column], ENTER, not_first_row | (column > 0),
+            )
     for i in range(len(rounds))[1:2]:
         hear(i)
 
     @pl.when(chip > 0)
     def _():
-        enter_in[chip_column] = enter_out[chip_column]
-        await_bytes(enter_in.at[0 : side - 1], ENTER)
-
-    send(twin, enter_in, enter_other, SWAP, chip > 0)
-
-    @pl.when(chip > 0)
-    def _():
-        state[:, mine] = enter_in[...].reshape(state_size, share)
-        await_bytes(enter_other, SWAP)
-        state[:, others] = enter_other[...].reshape(state_size, share)
+        enter_in[core * side + chip_column] = enter_out[chip_column]
+        await_bytes(enter_in.at[0 : 2 * side - 1], ENTER)
+        for half in range(2):
+            part = enter_in[half * side : (half + 1) * side]
+            state[:, half * share : (half + 1) * share] = part.reshape(state_size, share)
 
     @pl.when(chip == 0)
     def _():
@@ -398,8 +395,7 @@
             vmem((share_rows, share), F32),
             vmem((share_rows, share), F32),
             vmem((side, share_rows, share), F32),
-            vmem((side, share_rows, share), F32),
-            vmem((side, share_rows, share), F32),
+            vmem((2 * side, share_rows, share), F32),
             vmem((chunks, CHUNK), F32),
             vmem((nh, chunks, CHUNK), F32),
             pltpu.SemaphoreType.DMA((7,)),

time: 35 us -> 35 us (level)
  the two profiles are of different devices: /device:TPU:7 before, /device:TPU:6 now
where the time goes in v9:
time: 35 us; the launch traced here: 34.8 us
  Pallas kernels  34.8 us (99%)
    pallas_call x1, Pallas kernels, on_device(): pl.pallas_call(functools.partial(kernel, nh, nc, heads * nh // groups), o...  33.7 us
    pallas_call x1, Pallas kernels, on_device(): pl.pallas_call(normalize, out_shape=jax.ShapeDtypeStruct((tokens, lanes),...  1.14 us

profile of v9, /device:TPU:6, one launch (start us, length us, event | category | flops | bytes accessed | tf_op | source)
XLA Modules:
  0.0 34.8 jit_solution(2718813565753065100)
XLA Ops:
  0.0 0.0 copy-start
  0.0 33.7 %shard_map.82 = (f32[1024,512]{1,0:T(8,128)S(1)}, f32[8,128]{1,0:T(8,128)S(1)}) custom-call(s32[16]{0:T(128)} %lengths_hbm.1, f32[8]{0:T(128)} %skip_hbm.1, bf16[1024,512]{1,0:T(8,128)(2,1)} %x_hbm.1, bf16[1024,512]{1,0:T(8,128)(2,1)} %z_hbm.1, bf16[1024,1024]{1,0:T(8,128)(2,1)} %b_hbm.1, bf16[1024,1024]{1,0:T(8,128)(2,1)} %c_hbm.1, f32[8,1024]{1,0:T(8,128)} %bitcast.3), custom_call_target="tpu_custom_call" | custom-call | tf_op jit(solution)/shard_map/pallas_call | solution.py:359
  33.7 0.0 copy-done
  33.7 1.1 %shard_map.83 = bf16[1024,512]{1,0:T(8,128)(2,1)} custom-call(f32[1024,512]{1,0:T(8,128)S(1)} %get-tuple-element.7.gated, f32[8,128]{1,0:T(8,128)S(1)} %get-tuple-element.8.scales, f32[1,512]{1,0:T(1,128)S(1)} %bitcast.2), custom_call_target="tpu_custom_call" | custom-call | tf_op jit(solution)/shard_map/pallas_call | solution.py:413
Async XLA Ops:
  0.0 33.7 %copy-start = (f32[512]{0:T(512)S(1)}, f32[512]{0:T(512)}, u32[]{:S(2)}) copy-start(f32[512]{0:T(512)} %param.15) | copy-start | bytes 6148

commit v10 on v9

--- a/solution.py
+++ b/solution.py
@@ -57,7 +57,7 @@
         pltpu.make_async_copy(skip_hbm, skip, load_sem.at[5]),
         pltpu.make_async_copy(lengths_hbm, lengths, load_sem.at[6]),
     ]
-    for i in (6, 0, 1, 2, 3, 4, 5):
+    for i in (6, 0, 1, 2):
         loads[i].start()
 
     barrier = pltpu.get_barrier_semaphore()
@@ -177,6 +177,8 @@
     for k in range(chunks):
         b_turned[k] = b[k * CHUNK : (k + 1) * CHUNK, :].T
     loads[2].wait()
+    for i in (3, 4, 5):
+        loads[i].start()
     mine = pl.ds(pl.multiple_of(core * share, share), share)
     others = pl.ds(pl.multiple_of((1 - core) * share, share), share)
     for half, part, which in ((1 - core, others, FIRST_HALF), (core, mine, SECOND_HALF)):

time: 35 us -> 35 us (level)
  no operation moved by 1% of the time
where the time goes in v10:
time: 35 us; the launch traced here: 34.8 us
  Pallas kernels  34.8 us (99%)
    pallas_call x1, Pallas kernels, on_device(): pl.pallas_call(functools.partial(kernel, nh, nc, heads * nh // groups), o...  33.7 us
    pallas_call x1, Pallas kernels, on_device(): pl.pallas_call(normalize, out_shape=jax.ShapeDtypeStruct((tokens, lanes),...  1.14 us

profile of v10, /device:TPU:6, one launch (start us, length us, event | category | flops | bytes accessed | tf_op | source)
XLA Modules:
  0.0 34.8 jit_solution(12409294287165792407)
XLA Ops:
  0.0 0.0 copy-start
  0.0 33.7 %shard_map.82 = (f32[1024,512]{1,0:T(8,128)S(1)}, f32[8,128]{1,0:T(8,128)S(1)}) custom-call(s32[16]{0:T(128)} %lengths_hbm.1, f32[8]{0:T(128)} %skip_hbm.1, bf16[1024,512]{1,0:T(8,128)(2,1)} %x_hbm.1, bf16[1024,512]{1,0:T(8,128)(2,1)} %z_hbm.1, bf16[1024,1024]{1,0:T(8,128)(2,1)} %b_hbm.1, bf16[1024,1024]{1,0:T(8,128)(2,1)} %c_hbm.1, f32[8,1024]{1,0:T(8,128)} %bitcast.3), custom_call_target="tpu_custom_call" | custom-call | tf_op jit(solution)/shard_map/pallas_call | solution.py:361
  33.7 0.0 copy-done
  33.7 1.1 %shard_map.83 = bf16[1024,512]{1,0:T(8,128)(2,1)} custom-call(f32[1024,512]{1,0:T(8,128)S(1)} %get-tuple-element.7.gated, f32[8,128]{1,0:T(8,128)S(1)} %get-tuple-element.8.scales, f32[1,512]{1,0:T(1,128)S(1)} %bitcast.2), custom_call_target="tpu_custom_call" | custom-call | tf_op jit(solution)/shard_map/pallas_call | solution.py:415
Async XLA Ops:
  0.0 33.7 %copy-start = (f32[512]{0:T(512)S(1)}, f32[512]{0:T(512)}, u32[]{:S(2)}) copy-start(f32[512]{0:T(512)} %param.15) | copy-start | bytes 6148
